TPU v7x, 32 devices: a whole 2x2x4 slice. The times are simulated.
32 devices in a mesh: dp: 8 (over z, y), tensor: 4 (over x, core).
Axes of the slice: x: 2, y: 2, z: 4, core: 2. Of those that a mesh axis runs over, the one named last changes fastest.
Arguments:
- tokens: bfloat16 [8, 512, 768], P('dp'), as said below
- cotangent: bfloat16 [8, 512, 768], P('dp'), may hold values from -6 to 6
- lengths: int32 [8], P('dp'), may hold values from 128 to 512, as said below
- in_weight: float32 [7, 768, 768], P(None, 'dp', 'tensor'), as said below
- out_weight: float32 [5, 768, 768], P(None, 'tensor', 'dp'), may hold values from -0.4375 to 0.4375
- in_bias: float32 [6, 768], P(None, 'tensor'), may hold values from -3 to 3
- norm_vec: float32 [6, 768], replicated, may hold values from 0.1 to 1.9
- in_moments: float32 [2, 7, 768, 768], P(None, None, 'dp', 'tensor'), as said below
- out_moments: float32 [2, 5, 768, 768], P(None, None, 'tensor', 'dp'), as said below
- bias_moments: float32 [2, 6, 768], P(None, None, 'tensor'), as said below
- norm_moments: float32 [2, 6, 768], replicated, as said below
Outputs:
- output: bfloat16 [8, 512, 768], P('dp')
- grad_input: bfloat16 [8, 512, 768], P('dp')
- in_grad: float32 [7, 768, 768], P(None, 'dp', 'tensor')
- out_grad: float32 [5, 768, 768], P(None, 'tensor', 'dp')
- bias_grad: float32 [6, 768], P(None, 'tensor')
- norm_grad: float32 [6, 768], replicated
- new_in_weight: float32 [7, 768, 768], P(None, 'dp', 'tensor')
- new_out_weight: float32 [5, 768, 768], P(None, 'tensor', 'dp')
- new_in_bias: float32 [6, 768], P(None, 'tensor')
- new_norm_vec: float32 [6, 768], replicated
- new_in_moments: float32 [2, 7, 768, 768], P(None, None, 'dp', 'tensor')
- new_out_moments: float32 [2, 5, 768, 768], P(None, None, 'tensor', 'dp')
- new_bias_moments: float32 [2, 6, 768], P(None, None, 'tensor')
- new_norm_moments: float32 [2, 6, 768], replicated
Inputs may be any that keep to these rules, and one draw needn't show every extreme that they name: `lengths`: each sequence's live tokens come first; the first sequence is full, with 512 live tokens. `tokens`: entries lie within -6 and 6. `in_weight`: entries lie within -6 / sqrt(768) and 6 / sqrt(768). `in_moments`: second moments (index 1) are positive. `out_moments`: second moments (index 1) are positive. `bias_moments`: second moments (index 1) are positive. `norm_moments`: second moments (index 1) are positive.
All inputs are finite; a program needn't handle non-finite values.
Results may differ from a plain program's by a relative error of at most 0.023.
Values may be sent and summed in bfloat16 or wider, within the bound.
A program may use at most 128 MiB of HBM per device.

v0:
```python
import jax
import jax.numpy as jnp
from jax import lax
from jax.sharding import PartitionSpec as P

HDIM = 64


norm_eps = 1e-12
masked_score = -1e30
learn_rate = 0.005
beta_first = 0.9
beta_second = 0.999
adam_eps = 1e-08
weight_decay = 0.01
step_count = 2.0
root_half = 0.7071067811865476
normal_peak = 0.3989422804014327


def matmul(left_op, right_op):
    return jnp.dot(left_op, right_op, preferred_element_type=jnp.float32)


def inner_rows(left_op, right_op):
    return lax.dot_general(
        left_op, right_op, (((0,), (0,)), ((), ())), preferred_element_type=jnp.float32
    )


def times_transposed(left_op, right_op):
    return lax.dot_general(
        left_op, right_op, (((1,), (1,)), ((), ())), preferred_element_type=jnp.float32
    )


def layer_norm(summed_rows, gain_vec, shift_vec):
    center = jnp.mean(summed_rows, -1, keepdims=True)
    offset = summed_rows - center
    inverse = lax.rsqrt(jnp.mean(offset * offset, -1, keepdims=True) + norm_eps)
    normed = offset * inverse
    return (normed * gain_vec + shift_vec, normed, inverse)


def norm_back(upstream, normed, inverse, gain_vec):
    scaled = upstream * gain_vec
    return inverse * (
        scaled
        - jnp.mean(scaled, -1, keepdims=True)
        - normed * jnp.mean(scaled * normed, -1, keepdims=True)
    )


def gelu_value(pre_act):
    return 0.5 * pre_act * (1.0 + jax.scipy.special.erf(pre_act * root_half))


def gelu_slope(pre_act):
    return (
        0.5 * (1.0 + jax.scipy.special.erf(pre_act * root_half))
        + pre_act * jnp.exp(-0.5 * pre_act * pre_act) * normal_peak
    )


def score_block(query_heads, key_heads, length):
    seq_len = query_heads.shape[0]
    scale_factor = query_heads.shape[-1] ** (-0.5)
    scores = (
        jnp.einsum("qhe,khe->hqk", query_heads, key_heads, preferred_element_type=jnp.float32)
        * scale_factor
    )
    usable = lax.broadcasted_iota(jnp.int32, (1, 1, seq_len), 2) < length
    return jnp.where(usable, scores, masked_score)


def attend_forward(operands):
    query_heads, key_heads, value_heads, length = operands
    scores = score_block(query_heads, key_heads, length)
    highest = jnp.max(scores, -1, keepdims=True)
    log_total = highest + jnp.log(jnp.sum(jnp.exp(scores - highest), -1, keepdims=True))
    probs_low = jnp.exp(scores - log_total).astype(jnp.bfloat16)
    mixed_heads = jnp.einsum(
        "hqk,khe->qhe", probs_low, value_heads, preferred_element_type=jnp.float32
    )
    return (mixed_heads.astype(jnp.bfloat16), log_total)


def attend_backward(operands):
    query_heads, key_heads, value_heads, grad_heads, log_total, length = operands
    scale_factor = query_heads.shape[-1] ** (-0.5)
    scores = score_block(query_heads, key_heads, length)
    probs = jnp.exp(scores - log_total)
    probs_low = probs.astype(jnp.bfloat16)
    grad_probs = jnp.einsum(
        "qhe,khe->hqk", grad_heads, value_heads, preferred_element_type=jnp.float32
    )
    row_dot = jnp.sum(probs * grad_probs, -1, keepdims=True)
    grad_scores = (probs * (grad_probs - row_dot) * scale_factor).astype(jnp.bfloat16)
    grad_query = jnp.einsum(
        "hqk,khe->qhe", grad_scores, key_heads, preferred_element_type=jnp.float32
    )
    grad_keys = jnp.einsum(
        "hqk,qhe->khe", grad_scores, query_heads, preferred_element_type=jnp.float32
    )
    grad_values = jnp.einsum(
        "hqk,qhe->khe", probs_low, grad_heads, preferred_element_type=jnp.float32
    )
    return (grad_query, grad_keys, grad_values)


def adam_update(param, grad, moments, decay):
    first = beta_first * moments[0] + (1.0 - beta_first) * grad
    second = beta_second * moments[1] + (1.0 - beta_second) * grad * grad
    first_hat = first / (1.0 - beta_first**step_count)
    second_hat = second / (1.0 - beta_second**step_count)
    new_param = param - learn_rate * (first_hat / (jnp.sqrt(second_hat) + adam_eps) + decay * param)
    return (new_param, jnp.stack([first, second]))


def local(
    tokens,
    cotangent,
    lengths,
    in_weight,
    out_weight,
    in_bias,
    norm_vec,
    in_moments,
    out_moments,
    bias_moments,
    norm_moments,
):
    seq_count, seq_len, width = tokens.shape
    row_count = seq_count * seq_len
    in_full, out_full = (
        lax.all_gather(in_weight.astype(jnp.bfloat16), "dp", axis=1, tiled=True),
        lax.all_gather(out_weight.astype(jnp.bfloat16), "dp", axis=2, tiled=True),
    )
    group_width = in_full.shape[2]
    heads_here = group_width // HDIM
    w_query, w_key, w_value = (in_full[0], in_full[1], in_full[2])
    w_up = in_full[3:7]
    w_proj = out_full[0]
    w_down = out_full[1:5]
    bias_up = in_bias[2:6]

    def split_heads(flat_rows):
        return flat_rows.reshape(seq_count, seq_len, heads_here, HDIM)

    flat_tokens = tokens.reshape(row_count, width)
    query = (matmul(flat_tokens, w_query) + in_bias[0]).astype(jnp.bfloat16)
    keys_low = matmul(flat_tokens, w_key).astype(jnp.bfloat16)
    values_low = (matmul(flat_tokens, w_value) + in_bias[1]).astype(jnp.bfloat16)
    mixed_heads, log_total = lax.map(
        attend_forward,
        (split_heads(query), split_heads(keys_low), split_heads(values_low), lengths),
    )
    mixed_flat = mixed_heads.reshape(row_count, group_width)
    attn_out = lax.psum(matmul(mixed_flat, w_proj).astype(jnp.bfloat16), "tensor").astype(
        jnp.float32
    )
    hidden, normed_one, inverse_one = layer_norm(
        flat_tokens.astype(jnp.float32) + attn_out + norm_vec[0], norm_vec[1], norm_vec[2]
    )
    hidden_low = hidden.astype(jnp.bfloat16)
    pre_act = (
        jnp.einsum("rd,kdj->rkj", hidden_low, w_up, preferred_element_type=jnp.float32) + bias_up
    )
    act_low = gelu_value(pre_act).astype(jnp.bfloat16)
    ffn_part = jnp.einsum("rkj,kjd->rd", act_low, w_down, preferred_element_type=jnp.float32)
    ffn_out = lax.psum(ffn_part.astype(jnp.bfloat16), "tensor").astype(jnp.float32)
    out_rows, normed_two, inverse_two = layer_norm(
        hidden + ffn_out + norm_vec[3], norm_vec[4], norm_vec[5]
    )
    positions = lax.broadcasted_iota(jnp.int32, (seq_count, seq_len), 1)
    live_rows = (positions < lengths[:, None]).astype(jnp.float32).reshape(row_count, 1)
    grad_out = cotangent.reshape(row_count, width).astype(jnp.float32) * live_rows
    grad_two = norm_back(grad_out, normed_two, inverse_two, norm_vec[4])
    grad_two_low = grad_two.astype(jnp.bfloat16)
    grad_down = jnp.einsum("rkj,rd->kjd", act_low, grad_two_low, preferred_element_type=jnp.float32)
    grad_act = jnp.einsum("rd,kjd->rkj", grad_two_low, w_down, preferred_element_type=jnp.float32)
    grad_pre = grad_act * gelu_slope(pre_act)
    grad_pre_low = grad_pre.astype(jnp.bfloat16)
    grad_up = jnp.einsum(
        "rd,rkj->kdj", hidden_low, grad_pre_low, preferred_element_type=jnp.float32
    )
    back_part = jnp.einsum("rkj,kdj->rd", grad_pre_low, w_up, preferred_element_type=jnp.float32)
    grad_hidden = grad_two + lax.psum(back_part.astype(jnp.bfloat16), "tensor").astype(jnp.float32)
    grad_one = norm_back(grad_hidden, normed_one, inverse_one, norm_vec[1])
    grad_one_low = grad_one.astype(jnp.bfloat16)
    grad_proj = inner_rows(mixed_flat, grad_one_low)
    grad_mixed = times_transposed(grad_one_low, w_proj).astype(jnp.bfloat16)
    grad_query, grad_keys, grad_values = lax.map(
        attend_backward,
        (
            split_heads(query),
            split_heads(keys_low),
            split_heads(values_low),
            split_heads(grad_mixed),
            log_total,
            lengths,
        ),
    )
    grad_query = grad_query.reshape(row_count, group_width)
    grad_keys = grad_keys.reshape(row_count, group_width)
    grad_values = grad_values.reshape(row_count, group_width)
    query_grad_low = grad_query.astype(jnp.bfloat16)
    keys_grad_low = grad_keys.astype(jnp.bfloat16)
    values_grad_low = grad_values.astype(jnp.bfloat16)
    input_part = (
        times_transposed(query_grad_low, w_query)
        + times_transposed(keys_grad_low, w_key)
        + times_transposed(values_grad_low, w_value)
    )
    grad_input = grad_one + lax.psum(input_part.astype(jnp.bfloat16), "tensor").astype(jnp.float32)
    grad_in = jnp.concatenate(
        [
            jnp.stack(
                [
                    inner_rows(flat_tokens, query_grad_low),
                    inner_rows(flat_tokens, keys_grad_low),
                    inner_rows(flat_tokens, values_grad_low),
                ]
            ),
            grad_up,
        ],
        0,
    )
    grad_outw = jnp.concatenate([grad_proj[None], grad_down], 0)
    grad_bias = jnp.concatenate(
        [jnp.stack([jnp.sum(grad_query, 0), jnp.sum(grad_values, 0)]), jnp.sum(grad_pre, 0)], 0
    )
    grad_norm = jnp.stack(
        [
            jnp.sum(grad_one, 0),
            jnp.sum(grad_hidden * normed_one, 0),
            jnp.sum(grad_hidden, 0),
            jnp.sum(grad_two, 0),
            jnp.sum(grad_out * normed_two, 0),
            jnp.sum(grad_out, 0),
        ]
    )
    in_total, out_total, bias_total, norm_total = lax.psum(
        (grad_in, grad_outw, grad_bias, grad_norm), "dp"
    )
    owner = lax.axis_index("dp")
    in_rows = in_weight.shape[1]
    out_cols = out_weight.shape[2]
    in_share = lax.dynamic_slice_in_dim(in_total, owner * in_rows, in_rows, 1)
    out_share = lax.dynamic_slice_in_dim(out_total, owner * out_cols, out_cols, 2)
    new_in_weight, new_in_moments = adam_update(in_weight, in_share, in_moments, weight_decay)
    new_out_weight, new_out_moments = adam_update(out_weight, out_share, out_moments, weight_decay)
    new_in_bias, new_bias_moments = adam_update(in_bias, bias_total, bias_moments, 0.0)
    new_norm_vec, new_norm_moments = adam_update(norm_vec, norm_total, norm_moments, 0.0)
    output = out_rows.astype(jnp.bfloat16).reshape(seq_count, seq_len, width)
    grad_tokens = grad_input.astype(jnp.bfloat16).reshape(seq_count, seq_len, width)
    return (
        output,
        grad_tokens,
        in_share,
        out_share,
        bias_total,
        norm_total,
        new_in_weight,
        new_out_weight,
        new_in_bias,
        new_norm_vec,
        new_in_moments,
        new_out_moments,
        new_bias_moments,
        new_norm_moments,
    )


def solution(mesh):
    in_specs = (
        P("dp", None, None),
        P("dp", None, None),
        P("dp"),
        P(None, "dp", "tensor"),
        P(None, "tensor", "dp"),
        P(None, "tensor"),
        P(),
        P(None, None, "dp", "tensor"),
        P(None, None, "tensor", "dp"),
        P(None, None, "tensor"),
        P(),
    )
    out_specs = (
        P("dp", None, None),
        P("dp", None, None),
        P(None, "dp", "tensor"),
        P(None, "tensor", "dp"),
        P(None, "tensor"),
        P(),
        P(None, "dp", "tensor"),
        P(None, "tensor", "dp"),
        P(None, "tensor"),
        P(),
        P(None, None, "dp", "tensor"),
        P(None, None, "tensor", "dp"),
        P(None, None, "tensor"),
        P(),
    )
    return jax.shard_map(local, mesh=mesh, in_specs=in_specs, out_specs=out_specs, check_vma=False)
```

profile of v0, /device:TPU:0, one launch (start us, length us, event | category | flops | bytes accessed | tf_op | source)
XLA Modules:
  0.0 594.2 jit_solution(6022142361547197899)
XLA Ops:
  11.3 62.3 %all-gather.5.cloned.1.call-done = bf16[5,192,768]{1,0,2:T(8,128)(2,1)} async-done(((bf16[5,192,96]{1,0,2:T(8,128)(2,1)}), bf16[5,192,768]{1,0,2:T(8,128)(2,1)}) %all-gather.5.cloned.1.call-update) | async-done | bytes 1474576 | tf_op jit(solution)/shard_map/all_gather | solution.py:137
  73.5 2.4 slice.97
  77.6 57.4 %all-gather.3.cloned.1.call-done = bf16[7,768,192]{2,0,1:T(8,128)(2,1)} async-done(((bf16[7,96,192]{2,0,1:T(8,128)(2,1)}), bf16[7,768,192]{2,0,1:T(8,128)(2,1)}) %all-gather.3.cloned.1.call-update) | async-done | bytes 2064400 | tf_op jit(solution)/shard_map/all_gather | solution.py:136
  135.0 6.1 %fusion.97 = (bf16[1,768,192]{2,0,1:T(2,128)(2,1)S(1)}, bf16[1,768,192]{2,0,1:T(2,128)(2,1)S(1)}, bf16[1,768,192]{2,0,1:T(2,128)(2,1)S(1)}) fusion(bf16[7,768,192]{2,0,1:T(8,128)(2,1)} %all-gather.3.cloned.1.call-done), kind=kLoop, calls=%fused_computation.162 | loop fusion | bytes 1769472 | tf_op jit(solution)/shard_map/slice | solution.py:141
  149.5 2.8 slice.99
  152.3 2.2 copy.141
  154.5 2.7 slice.98
  159.4 23.8 %all-reduce.8.cloned.1.call-done = bf16[512,768]{1,0:T(8,128)(2,1)} async-done(((bf16[512,768]{1,0:T(8,128)(2,1)}), bf16[512,768]{1,0:T(8,128)(2,1)}) %all-reduce.8.cloned.1.call-update) | async-done | bytes 786448 | tf_op jit(solution)/shard_map/psum | solution.py:159
  190.2 34.9 %all-reduce.10.cloned.1.call-done = bf16[512,768]{1,0:T(8,128)(2,1)} async-done(((bf16[512,768]{1,0:T(8,128)(2,1)}), bf16[512,768]{1,0:T(8,128)(2,1)}) %all-reduce.10.cloned.1.call-update) | async-done | bytes 786448 | tf_op jit(solution)/shard_map/psum | solution.py:171
  235.7 3.4 fusion.41
  239.1 2.5 convolution_bitcast_fusion
  241.6 29.2 %all-reduce.12.cloned.1.call-done = bf16[512,768]{1,0:T(8,128)(2,1)} async-done(((bf16[512,768]{1,0:T(8,128)(2,1)}), bf16[512,768]{1,0:T(8,128)(2,1)}) %all-reduce.12.cloned.1.call-update) | async-done | bytes 786448 | tf_op jit(solution)/shard_map/psum | solution.py:188
  270.9 2.8 multiply_reduce_fusion.1
  273.7 2.8 fusion.95
  277.5 2.4 fusion.107
  279.8 7.2 %fusion.99 = (f32[3,64]{1,0:T(4,128)}, bf16[512,3,64]{0,2,1:T(8,128)(2,1)S(1)}) fusion(bf16[512,3,64]{0,2,1:T(8,128)(2,1)S(1)} %bitcast.222, f32[3,512,512]{1,2,0:T(8,128)} %fusion.107, f32[3,512]{1,0:T(4,128)S(1)} %log_add_fusion, f32[3,512,512]{1,2,0:T(8,128)} %copy-done.3, pred[512]{0:T(512)(128)(4,1)S(1)} %iota_compare_fusion), kind=kOutput, calls=%fused_computation.164 | convolution fusion | flops 109512512 | bytes 6692096 | tf_op jit(solution)/shard_map/while/body/eval_jaxpr/hqk,khe->qhe/dot_general | solution.py:99
  287.0 6.6 %fusion.35 = bf16[3,64,512]{2,1,0:T(8,128)(2,1)S(1)} fusion(bf16[512,3,64]{0,2,1:T(8,128)(2,1)S(1)} %bitcast.232, f32[3,512,512]{1,2,0:T(8,128)} %fusion.107, f32[3,512,512]{1,2,0:T(8,128)} %copy-done.3, f32[3,512]{1,0:T(4,128)S(1)} %log_add_fusion, pred[512]{0:T(512)(128)(4,1)S(1)} %iota_compare_fusion), kind=kOutput, calls=%fused_computation.65 | convolution fusion | flops 109414400 | bytes 6691328 | tf_op jit(solution)/shard_map/while/body/eval_jaxpr/hqk,qhe->khe/dot_general | solution.py:102
  293.7 3.5 fusion.100
  304.3 3.8 pad_maximum_fusion.1
  308.1 2.3 pad_maximum_fusion
  312.6 2.3 fusion.98
  318.0 37.5 %all-reduce = (f32[6,192]{1,0:T(8,128)S(1)}, f32[6,768]{1,0:T(8,128)S(1)}) all-reduce(f32[6,192]{1,0:T(8,128)S(1)} %pad_maximum_fusion.6, f32[6,768]{1,0:T(8,128)S(1)} %stack.83), channel_id=1, replica_groups=mesh['dp'=8,'tensor'=4] {'dp'}, use_global_device_ids=true, to_apply=%region_20.21 | all-reduce | flops 5760 | bytes 46080 | tf_op jit(solution)/shard_map/psum | solution.py:243
  360.2 214.8 %all-reduce.16.cloned.1.call-done = (f32[7,768,192]{1,2,0:T(8,128)}, f32[5,192,768]{2,1,0:T(8,128)}) async-done(((f32[7,768,192]{1,2,0:T(8,128)}, f32[5,192,768]{2,1,0:T(8,128)}), (f32[7,768,192]{1,2,0:T(8,128)}, f32[5,192,768]{2,1,0:T(8,128)})) %all-reduce.16.cloned.1.call-update) | async-done | bytes 7077904 | tf_op jit(solution)/shard_map/psum | solution.py:243
  579.4 2.4 copy.128
  (205 shorter events, 60.4 us)
Async XLA Ops:
  7.2 66.3 %all-gather.5.cloned.1.call-start = ((), (), s32[]{:S(2)}) async-start(), calls=%async_computation.1 | async-start | bytes 3538944 | tf_op jit(solution)/shard_map/all_gather | solution.py:137
  8.4 2.9 copy-start.43
  9.5 125.5 %all-gather.3.cloned.1.call-start = ((), (), s32[]{:S(2)}) async-start(), calls=%async_computation | async-start | bytes 3538944 | tf_op jit(solution)/shard_map/all_gather | solution.py:136
  10.5 172.7 %all-reduce.8.cloned.1.call-start = ((), (), s32[]{:S(2)}) async-start(), calls=%async_computation.2 | async-start | bytes 1572864 | tf_op jit(solution)/shard_map/psum | solution.py:159
  149.4 75.7 %all-reduce.10.cloned.1.call-start = ((), (), s32[]{:S(2)}) async-start(), calls=%async_computation.3 | async-start | bytes 1572864 | tf_op jit(solution)/shard_map/psum | solution.py:171
  189.9 80.9 %all-reduce.12.cloned.1.call-start = ((), (), s32[]{:S(2)}) async-start(), calls=%async_computation.4 | async-start | bytes 1572864 | tf_op jit(solution)/shard_map/psum | solution.py:188
  230.6 40.2 %copy-start.1 = (f32[512,768]{1,0:T(8,128)}, f32[512,768]{1,0:T(8,128)S(1)}, u32[]{:S(2)}) copy-start(f32[512,768]{1,0:T(8,128)S(1)} %get-tuple-element.165) | copy-start | bytes 4718596
  235.7 122.3 %all-reduce.14.cloned.1.call-start = ((), (), s32[]{:S(2)}) async-start(), calls=%async_computation.5 | async-start | bytes 1572864 | tf_op jit(solution)/shard_map/psum | solution.py:215
  235.7 3.4 copy-start.55
  279.8 7.2 %copy-start.39 = (bf16[512,192]{0,1:T(8,128)(2,1)S(1)}, bf16[512,192]{0,1:T(8,128)(2,1)}, u32[]{:S(2)}) copy-start(bf16[512,192]{0,1:T(8,128)(2,1)} %copy-done.38) | copy-start | bytes 589828
  287.0 11.8 %copy-start.34 = (bf16[512,3,64]{0,2,1:T(8,128)(2,1)}, bf16[512,3,64]{0,2,1:T(8,128)(2,1)S(1)}, u32[]{:S(2)}) copy-start(bf16[512,3,64]{0,2,1:T(8,128)(2,1)S(1)} %get-tuple-element.174) | copy-start | bytes 589828
  293.7 3.5 copy-start.35
  304.2 3.9 copy-start.14
  304.2 270.8 %all-reduce.16.cloned.1.call-start = ((), (), s32[]{:S(2)}) async-start(), calls=%async_computation.6 | async-start | bytes 14155776 | tf_op jit(solution)/shard_map/psum | solution.py:243
  304.2 3.8 copy-start.15
  314.9 2.9 copy-start.48
  314.9 2.9 copy-start.47
  314.9 2.9 copy-start.46
  314.9 2.9 copy-start.45
  314.9 3.0 copy-start.51
  314.9 41.8 %copy-start.41 = (f32[6,768]{1,0:T(8,128)S(1)}, f32[6,768]{1,0:T(8,128)}, u32[]{:S(2)}) copy-start(f32[6,768]{1,0:T(8,128)} %param.17) | copy-start | bytes 55300
  355.5 4.7 copy-start.44
  355.5 4.7 copy-start.50
  579.4 3.8 copy-start.17
  (39 other events, 72.2 us)
Sparse Core Ops, SparseCore 0:
  10.8 62.7 all-gather.4
  76.3 58.6 all-gather.2
  149.5 33.6 all-reduce.7
  190.0 35.0 all-reduce.9
  235.8 35.0 all-reduce.11
  304.3 35.0 all-reduce.13
  343.4 231.5 all-reduce.15
where the time goes:
time: 595 us; the launch traced here: 594 us
  waiting for transfers between devices  423 us (71%)
  matrix products  43.5 us (7%)
  local copies, waits for them, and re-layouts  43.2 us (7%)
  blocking collectives  37.5 us (6%)
  other arithmetic  31.4 us (5%)
  between operations  15.5 us (3%)
    psum x1, waiting for transfers between devices, local(): lax.psum((grad_in, grad_outw, grad_bias, grad_norm), 'dp')  215 us
    all_gather x1, waiting for transfers between devices, local(): lax.all_gather(out_weight.astype(jnp.bfloat16), 'dp', axis=2, tiled=True)  62.3 us
    all_gather x1, waiting for transfers between devices, local(): lax.all_gather(in_weight.astype(jnp.bfloat16), 'dp', axis=1, tiled=True)  57.4 us
    psum x1, blocking collectives, local(): lax.psum((grad_in, grad_outw, grad_bias, grad_norm), 'dp')  37.5 us
    psum x1, waiting for transfers between devices, local(): lax.psum(ffn_part.astype(jnp.bfloat16), 'tensor').astype(jnp.float32)  34.9 us
    psum x1, waiting for transfers between devices, local(): lax.psum(back_part.astype(jnp.bfloat16), 'tensor').astype(jnp.float32)  29.2 us
    unnamed x126, local copies, waits for them, and re-layouts  24.5 us
    psum x1, waiting for transfers between devices, local(): lax.psum(matmul(mixed_flat, w_proj).astype(jnp.bfloat16), 'tensor')  23.8 us
  transfers between devices with their start and end apart: 7, of which 6 were waited for; matrix products, arithmetic and copies ran while one was open for 6% of the time, Pallas kernels for 0%

commit v1 on v0

--- a/solution.py
+++ b/solution.py
@@ -1,6 +1,10 @@
+import functools
+
 import jax
 import jax.numpy as jnp
 from jax import lax
+from jax.experimental import pallas as pl
+from jax.experimental.pallas import tpu as pltpu
 from jax.sharding import PartitionSpec as P
 
 HDIM = 64
@@ -16,6 +20,287 @@
 step_count = 2.0
 root_half = 0.7071067811865476
 normal_peak = 0.3989422804014327
+
+
+RING = 8
+MESH = pl.DeviceIdType.MESH
+
+
+def ring_place(index):
+    depth, side = index // 2, index % 2
+    return depth + side * (RING - 1 - 2 * depth)
+
+
+def ring_device(place):
+    side = place // (RING // 2)
+    depth = place + side * (RING - 1 - 2 * place)
+    return 2 * depth + side
+
+
+def ring_neighbours():
+    me = lax.axis_index("dp")
+    place = ring_place(me)
+    right = ring_device((place + 1) % RING)
+    left = ring_device((place + RING - 1) % RING)
+    return me, place, (right, left)
+
+
+def greet(axis, devices):
+    barrier = pltpu.get_barrier_semaphore()
+    for device in devices:
+        pl.semaphore_signal(barrier, inc=1, device_id={axis: device}, device_id_type=MESH)
+    pl.semaphore_wait(barrier, len(devices))
+
+
+PIECES = 2
+
+
+def gather_kernel(share_ref, full_ref, local_sem, send_sem, recv_sem):
+    me, place, targets = ring_neighbours()
+    rows, columns = share_ref.shape
+    piece_rows, half = rows // PIECES, columns // 2
+
+    def full_at(owner, piece, way):
+        start = pl.multiple_of(owner * rows + piece * piece_rows, piece_rows)
+        return full_ref.at[pl.ds(start, piece_rows), pl.ds(way * half, half)]
+
+    own_start = pl.multiple_of(me * rows, rows)
+    own = pltpu.make_async_copy(share_ref, full_ref.at[pl.ds(own_start, rows)], local_sem)
+    own.start()
+    greet("dp", targets)
+    copies = {}
+    for step in range(RING - 1):
+        for piece in range(PIECES):
+            for way in range(2):
+                if step:
+                    copies[step - 1, piece, way].wait_recv()
+                shift = RING - step if way == 0 else step
+                owner = ring_device((place + shift) % RING)
+                target = full_at(owner, piece, way)
+                source = target
+                if step == 0:
+                    source = share_ref.at[
+                        pl.ds(piece * piece_rows, piece_rows), pl.ds(way * half, half)
+                    ]
+                copy = pltpu.make_async_remote_copy(
+                    src_ref=source,
+                    dst_ref=target,
+                    send_sem=send_sem.at[step, piece, way],
+                    recv_sem=recv_sem.at[step, piece, way],
+                    device_id={"dp": targets[way]},
+                    device_id_type=MESH,
+                )
+                copy.start()
+                copies[step, piece, way] = copy
+    for (step, piece, way), copy in copies.items():
+        copy.wait_send()
+        if step == RING - 2:
+            copy.wait_recv()
+    own.wait()
+
+
+def ring_gather(share):
+    rows, columns = share.shape
+    return pl.pallas_call(
+        gather_kernel,
+        out_shape=jax.ShapeDtypeStruct((rows * RING, columns), share.dtype),
+        in_specs=[pl.BlockSpec(memory_space=pltpu.VMEM)],
+        out_specs=pl.BlockSpec(memory_space=pltpu.VMEM),
+        scratch_shapes=[
+            pltpu.SemaphoreType.DMA,
+            pltpu.SemaphoreType.DMA((RING - 1, PIECES, 2)),
+            pltpu.SemaphoreType.DMA((RING - 1, PIECES, 2)),
+        ],
+        compiler_params=pltpu.CompilerParams(collective_id=0, has_side_effects=True),
+    )(share)
+
+
+def scatter_kernel(
+    grad_ref,
+    small_ref,
+    share_ref,
+    small_out_ref,
+    arrived,
+    leaving,
+    small_slots,
+    send_sem,
+    recv_sem,
+    small_send,
+    small_recv,
+):
+    me, place, targets = ring_neighbours()
+    rows, columns = share_ref.shape
+    piece_rows, half = rows // PIECES, columns // 2
+    greet("dp", [(me + shift) % RING for shift in range(1, RING)])
+
+    def grad_at(owner, piece, way):
+        start = pl.multiple_of(owner * rows + piece * piece_rows, piece_rows)
+        return grad_ref.at[pl.ds(start, piece_rows), pl.ds(way * half, half)]
+
+    copies = {}
+    small_copies = []
+    for step in range(RING - 1):
+        for piece in range(PIECES):
+            for way in range(2):
+                shift = RING - 1 - step if way == 0 else 1 + step
+                source = grad_at(ring_device((place + shift) % RING), piece, way)
+                if step:
+                    copies[step - 1, piece, way].wait_recv()
+                    running = arrived[step - 1, piece, way].astype(jnp.float32)
+                    running += source[...].astype(jnp.float32)
+                    leaving[step, piece, way] = running.astype(jnp.bfloat16)
+                    source = leaving.at[step, piece, way]
+                copy = pltpu.make_async_remote_copy(
+                    src_ref=source,
+                    dst_ref=arrived.at[step, piece, way],
+                    send_sem=send_sem.at[step, piece, way],
+                    recv_sem=recv_sem.at[step, piece, way],
+                    device_id={"dp": targets[way]},
+                    device_id_type=MESH,
+                )
+                copy.start()
+                copies[step, piece, way] = copy
+        if step == 0:
+            for shift in range(1, RING):
+                copy = pltpu.make_async_remote_copy(
+                    src_ref=small_ref,
+                    dst_ref=small_slots.at[me],
+                    send_sem=small_send.at[shift - 1],
+                    recv_sem=small_recv.at[shift - 1],
+                    device_id={"dp": (me + shift) % RING},
+                    device_id_type=MESH,
+                )
+                copy.start()
+                small_copies.append(copy)
+    for piece in range(PIECES):
+        for way in range(2):
+            copies[RING - 2, piece, way].wait_recv()
+            total = arrived[RING - 2, piece, way].astype(jnp.float32)
+            total += grad_at(me, piece, way)[...].astype(jnp.float32)
+            share_ref[pl.ds(piece * piece_rows, piece_rows), pl.ds(way * half, half)] = total
+    for copy in small_copies:
+        copy.wait_recv()
+    small_slots[me] = small_ref[...]
+    small_total = small_slots[0]
+    for index in range(1, RING):
+        small_total += small_slots[index]
+    small_out_ref[...] = small_total
+    for copy in small_copies:
+        copy.wait_send()
+    for copy in copies.values():
+        copy.wait_send()
+
+
+def ring_scatter(grads, small):
+    rows, columns = grads.shape[0] // RING, grads.shape[1]
+    slot_shape = (RING - 1, PIECES, 2, rows // PIECES, columns // 2)
+    vmem = pl.BlockSpec(memory_space=pltpu.VMEM)
+    return pl.pallas_call(
+        scatter_kernel,
+        out_shape=(
+            jax.ShapeDtypeStruct((rows, columns), jnp.float32),
+            jax.ShapeDtypeStruct(small.shape, jnp.float32),
+        ),
+        in_specs=[vmem, vmem],
+        out_specs=(vmem, vmem),
+        scratch_shapes=[
+            pltpu.VMEM(slot_shape, jnp.bfloat16),
+            pltpu.VMEM(slot_shape, jnp.bfloat16),
+            pltpu.VMEM((RING,) + small.shape, jnp.float32),
+            pltpu.SemaphoreType.DMA(slot_shape[:3]),
+            pltpu.SemaphoreType.DMA(slot_shape[:3]),
+            pltpu.SemaphoreType.DMA((RING - 1,)),
+            pltpu.SemaphoreType.DMA((RING - 1,)),
+        ],
+        compiler_params=pltpu.CompilerParams(collective_id=1, has_side_effects=True),
+    )(grads, small)
+
+
+PARTS = 4
+
+
+def reduce_kernel(part_ref, sum_ref, near, chip_sum, far, total, send_sem, recv_sem):
+    me = lax.axis_index("tensor")
+    core = me % 2
+    partner = me + 1 - 2 * core
+    across = (me + 2) % 4
+    half = part_ref.shape[0] // 2
+    size = half // PARTS
+    greet("tensor", (partner, across))
+
+    def rows_of(side, piece):
+        return pl.ds(pl.multiple_of(side * half + piece * size, size), size)
+
+    def send(source, target, stage, piece, device):
+        copy = pltpu.make_async_remote_copy(
+            src_ref=source,
+            dst_ref=target,
+            send_sem=send_sem.at[stage, piece],
+            recv_sem=recv_sem.at[stage, piece],
+            device_id={"tensor": device},
+            device_id_type=MESH,
+        )
+        copy.start()
+        return copy
+
+    first = [
+        send(part_ref.at[rows_of(1 - core, piece)], near.at[piece], 0, piece, partner)
+        for piece in range(PARTS)
+    ]
+    second = []
+    for piece in range(PARTS):
+        first[piece].wait_recv()
+        chip = near[piece].astype(jnp.float32) + part_ref[rows_of(core, piece)].astype(jnp.float32)
+        chip_sum[piece] = chip.astype(jnp.bfloat16)
+        second.append(send(chip_sum.at[piece], far.at[piece], 1, piece, across))
+    third = []
+    for piece in range(PARTS):
+        second[piece].wait_recv()
+        both = chip_sum[piece].astype(jnp.float32) + far[piece].astype(jnp.float32)
+        total[piece] = both.astype(jnp.bfloat16)
+        third.append(send(total.at[piece], sum_ref.at[rows_of(core, piece)], 2, piece, partner))
+    for piece in range(PARTS):
+        third[piece].wait_recv()
+        sum_ref[rows_of(core, piece)] = total[piece]
+    for copy in first + second + third:
+        copy.wait_send()
+
+
+def tensor_sum(part, call):
+    part = part.astype(jnp.bfloat16)
+    if lax.axis_size("tensor") != 4 or part.shape[0] % 128:
+        return lax.psum(part, "tensor").astype(jnp.float32)
+    rows, columns = part.shape
+    slots = pltpu.VMEM((PARTS, rows // (2 * PARTS), columns), jnp.bfloat16)
+    vmem = pl.BlockSpec(memory_space=pltpu.VMEM)
+    return pl.pallas_call(
+        reduce_kernel,
+        out_shape=jax.ShapeDtypeStruct(part.shape, jnp.bfloat16),
+        in_specs=[vmem],
+        out_specs=vmem,
+        scratch_shapes=[
+            slots,
+            slots,
+            slots,
+            slots,
+            pltpu.SemaphoreType.DMA((3, PARTS)),
+            pltpu.SemaphoreType.DMA((3, PARTS)),
+        ],
+        compiler_params=pltpu.CompilerParams(collective_id=2 + call, has_side_effects=True),
+    )(part).astype(jnp.float32)
+
+
+def gather_weights(share):
+    if lax.axis_size("dp") == RING and share.shape[0] % 32 == 0:
+        return ring_gather(share)
+    return lax.all_gather(share, "dp", axis=0, tiled=True)
+
+
+def scatter_grads(grads, small):
+    if lax.axis_size("dp") == RING and grads.shape[0] % (32 * RING) == 0:
+        return ring_scatter(grads, small)
+    share = lax.psum_scatter(grads, "dp", scatter_dimension=0, tiled=True)
+    return share.astype(jnp.float32), lax.psum(small, "dp")
 
 
 def matmul(left_op, right_op):
@@ -132,43 +417,39 @@
 ):
     seq_count, seq_len, width = tokens.shape
     row_count = seq_count * seq_len
-    in_full, out_full = (
-        lax.all_gather(in_weight.astype(jnp.bfloat16), "dp", axis=1, tiled=True),
-        lax.all_gather(out_weight.astype(jnp.bfloat16), "dp", axis=2, tiled=True),
-    )
-    group_width = in_full.shape[2]
+    in_low = in_weight.astype(jnp.bfloat16)
+    out_low = out_weight.astype(jnp.bfloat16).swapaxes(1, 2)
+    share = jnp.concatenate(list(in_low[:3]) + [out_low[0]] + list(in_low[3:]) + list(out_low[1:]), 1)
+    full = gather_weights(share)
+    group_width = in_weight.shape[2]
     heads_here = group_width // HDIM
-    w_query, w_key, w_value = (in_full[0], in_full[1], in_full[2])
-    w_up = in_full[3:7]
-    w_proj = out_full[0]
-    w_down = out_full[1:5]
-    bias_up = in_bias[2:6]
+    w_qkv = full[:, : 3 * group_width]
+    w_proj = full[:, 3 * group_width : 4 * group_width]
+    w_up = full[:, 4 * group_width : 8 * group_width]
+    w_down = full[:, 8 * group_width :]
+    bias_up = in_bias[2:6].reshape(1, 4 * group_width)
 
     def split_heads(flat_rows):
         return flat_rows.reshape(seq_count, seq_len, heads_here, HDIM)
 
     flat_tokens = tokens.reshape(row_count, width)
-    query = (matmul(flat_tokens, w_query) + in_bias[0]).astype(jnp.bfloat16)
-    keys_low = matmul(flat_tokens, w_key).astype(jnp.bfloat16)
-    values_low = (matmul(flat_tokens, w_value) + in_bias[1]).astype(jnp.bfloat16)
+    qkv = matmul(flat_tokens, w_qkv)
+    query = (qkv[:, :group_width] + in_bias[0]).astype(jnp.bfloat16)
+    keys_low = qkv[:, group_width : 2 * group_width].astype(jnp.bfloat16)
+    values_low = (qkv[:, 2 * group_width :] + in_bias[1]).astype(jnp.bfloat16)
     mixed_heads, log_total = lax.map(
         attend_forward,
         (split_heads(query), split_heads(keys_low), split_heads(values_low), lengths),
     )
     mixed_flat = mixed_heads.reshape(row_count, group_width)
-    attn_out = lax.psum(matmul(mixed_flat, w_proj).astype(jnp.bfloat16), "tensor").astype(
-        jnp.float32
-    )
+    attn_out = tensor_sum(times_transposed(mixed_flat, w_proj), 0)
     hidden, normed_one, inverse_one = layer_norm(
         flat_tokens.astype(jnp.float32) + attn_out + norm_vec[0], norm_vec[1], norm_vec[2]
     )
     hidden_low = hidden.astype(jnp.bfloat16)
-    pre_act = (
-        jnp.einsum("rd,kdj->rkj", hidden_low, w_up, preferred_element_type=jnp.float32) + bias_up
-    )
+    pre_act = matmul(hidden_low, w_up) + bias_up
     act_low = gelu_value(pre_act).astype(jnp.bfloat16)
-    ffn_part = jnp.einsum("rkj,kjd->rd", act_low, w_down, preferred_element_type=jnp.float32)
-    ffn_out = lax.psum(ffn_part.astype(jnp.bfloat16), "tensor").astype(jnp.float32)
+    ffn_out = tensor_sum(times_transposed(act_low, w_down), 1)
     out_rows, normed_two, inverse_two = layer_norm(
         hidden + ffn_out + norm_vec[3], norm_vec[4], norm_vec[5]
     )
@@ -177,19 +458,16 @@
     grad_out = cotangent.reshape(row_count, width).astype(jnp.float32) * live_rows
     grad_two = norm_back(grad_out, normed_two, inverse_two, norm_vec[4])
     grad_two_low = grad_two.astype(jnp.bfloat16)
-    grad_down = jnp.einsum("rkj,rd->kjd", act_low, grad_two_low, preferred_element_type=jnp.float32)
-    grad_act = jnp.einsum("rd,kjd->rkj", grad_two_low, w_down, preferred_element_type=jnp.float32)
+    grad_down = inner_rows(grad_two_low, act_low).astype(jnp.bfloat16)
+    grad_act = matmul(grad_two_low, w_down)
     grad_pre = grad_act * gelu_slope(pre_act)
     grad_pre_low = grad_pre.astype(jnp.bfloat16)
-    grad_up = jnp.einsum(
-        "rd,rkj->kdj", hidden_low, grad_pre_low, preferred_element_type=jnp.float32
-    )
-    back_part = jnp.einsum("rkj,kdj->rd", grad_pre_low, w_up, preferred_element_type=jnp.float32)
-    grad_hidden = grad_two + lax.psum(back_part.astype(jnp.bfloat16), "tensor").astype(jnp.float32)
+    grad_up = inner_rows(hidden_low, grad_pre_low).astype(jnp.bfloat16)
+    grad_hidden = grad_two + tensor_sum(times_transposed(grad_pre_low, w_up), 2)
     grad_one = norm_back(grad_hidden, normed_one, inverse_one, norm_vec[1])
     grad_one_low = grad_one.astype(jnp.bfloat16)
-    grad_proj = inner_rows(mixed_flat, grad_one_low)
-    grad_mixed = times_transposed(grad_one_low, w_proj).astype(jnp.bfloat16)
+    grad_proj = inner_rows(grad_one_low, mixed_flat).astype(jnp.bfloat16)
+    grad_mixed = matmul(grad_one_low, w_proj).astype(jnp.bfloat16)
     grad_query, grad_keys, grad_values = lax.map(
         attend_backward,
         (
@@ -204,33 +482,14 @@
     grad_query = grad_query.reshape(row_count, group_width)
     grad_keys = grad_keys.reshape(row_count, group_width)
     grad_values = grad_values.reshape(row_count, group_width)
-    query_grad_low = grad_query.astype(jnp.bfloat16)
-    keys_grad_low = grad_keys.astype(jnp.bfloat16)
-    values_grad_low = grad_values.astype(jnp.bfloat16)
-    input_part = (
-        times_transposed(query_grad_low, w_query)
-        + times_transposed(keys_grad_low, w_key)
-        + times_transposed(values_grad_low, w_value)
-    )
-    grad_input = grad_one + lax.psum(input_part.astype(jnp.bfloat16), "tensor").astype(jnp.float32)
-    grad_in = jnp.concatenate(
-        [
-            jnp.stack(
-                [
-                    inner_rows(flat_tokens, query_grad_low),
-                    inner_rows(flat_tokens, keys_grad_low),
-                    inner_rows(flat_tokens, values_grad_low),
-                ]
-            ),
-            grad_up,
-        ],
-        0,
-    )
-    grad_outw = jnp.concatenate([grad_proj[None], grad_down], 0)
-    grad_bias = jnp.concatenate(
-        [jnp.stack([jnp.sum(grad_query, 0), jnp.sum(grad_values, 0)]), jnp.sum(grad_pre, 0)], 0
-    )
-    grad_norm = jnp.stack(
+    qkv_grad_low = jnp.concatenate([grad_query, grad_keys, grad_values], 1).astype(jnp.bfloat16)
+    grad_input = grad_one + tensor_sum(times_transposed(qkv_grad_low, w_qkv), 3)
+    grad_qkv = inner_rows(flat_tokens, qkv_grad_low).astype(jnp.bfloat16)
+    grads = jnp.concatenate([grad_qkv, grad_proj, grad_up, grad_down], 1)
+    bias_rows = jnp.concatenate(
+        [jnp.sum(grad_query, 0), jnp.sum(grad_values, 0), jnp.sum(grad_pre, 0)]
+    ).reshape(6, group_width)
+    norm_rows = jnp.stack(
         [
             jnp.sum(grad_one, 0),
             jnp.sum(grad_hidden * normed_one, 0),
@@ -240,14 +499,13 @@
             jnp.sum(grad_out, 0),
         ]
     )
-    in_total, out_total, bias_total, norm_total = lax.psum(
-        (grad_in, grad_outw, grad_bias, grad_norm), "dp"
-    )
-    owner = lax.axis_index("dp")
-    in_rows = in_weight.shape[1]
-    out_cols = out_weight.shape[2]
-    in_share = lax.dynamic_slice_in_dim(in_total, owner * in_rows, in_rows, 1)
-    out_share = lax.dynamic_slice_in_dim(out_total, owner * out_cols, out_cols, 2)
+    small = jnp.pad(jnp.concatenate([norm_rows, bias_rows], 1), ((0, 2), (0, 64)))
+    share_total, small_total = scatter_grads(grads, small)
+    norm_total = small_total[:6, :width]
+    bias_total = small_total[:6, width : width + group_width]
+    blocks = [share_total[:, k * group_width : (k + 1) * group_width] for k in range(12)]
+    in_share = jnp.stack(blocks[:3] + blocks[4:8])
+    out_share = jnp.stack([blocks[3]] + blocks[8:]).swapaxes(1, 2)
     new_in_weight, new_in_moments = adam_update(in_weight, in_share, in_moments, weight_decay)
     new_out_weight, new_out_moments = adam_update(out_weight, out_share, out_moments, weight_decay)
     new_in_bias, new_bias_moments = adam_update(in_bias, bias_total, bias_moments, 0.0)

time: 595 us -> 261 us (0.44)
  waiting for transfers between devices: 423 us -> 0 us
  Pallas kernels: 0 us -> 153 us
  blocking collectives: 37.5 us -> 0 us
  between operations: 15.5 us -> 2.01 us
  local copies, waits for them, and re-layouts: 43.2 us -> 34.6 us
  other arithmetic: 31.4 us -> 23.6 us
    psum x5 -> x0, waiting for transfers between devices: 303 us -> none  [the longest x1 215 us: local(): lax.psum((grad_in, grad_outw, grad_bias, grad_norm), 'dp')]
    pallas_call x0 -> x6, Pallas kernels: none -> 153 us  [the longest x4 63.5 us: tensor_sum(): pl.pallas_call(reduce_kernel, out_shape=jax.ShapeDtypeStruct(part.shape,...]
    all_gather x2 -> x0, waiting for transfers between devices: 120 us -> none  [the longest x1 62.3 us: local(): lax.all_gather(out_weight.astype(jnp.bfloat16), 'dp', axis=2, tiled=True)]
    psum x1 -> x0, blocking collectives: 37.5 us -> none  [local(): lax.psum((grad_in, grad_outw, grad_bias, grad_norm), 'dp')]
    slice x6 -> x3, local copies, waits for them, and re-layouts: 14 us -> 1.51 us  [the longest x1 0.78 us: local(): query = (qkv[:, :group_width] + in_bias[0]).astype(jnp.bfloat16)]
    dot_general x5 -> x0, matrix products: 11.3 us -> none  [the longest x1 3.41 us: local(): jnp.einsum('rkj,rd->kjd', act_low, grad_two_low, preferred_element_type=j...]
    dot_general x4, matrix products: 2.52 us -> 10.2 us  [times_transposed(): lax.dot_general(left_op, right_op, (((1,), (1,)), ((), ())), preferred_el...]
    concatenate x0 -> x3, local copies, waits for them, and re-layouts: none -> 7.05 us  [the longest x1 6 us: local(): grads = jnp.concatenate([grad_qkv, grad_proj, grad_up, grad_down], 1)]
  transfers between devices with their start and end apart: 7 -> 0, of which waited for: 6 -> 0; matrix products, arithmetic and copies ran while one was open for 6% -> 0% of each run, Pallas kernels for 0% -> 0%
where the time goes in v1:
time: 261 us; the launch traced here: 259 us
  Pallas kernels  153 us (59%)
  matrix products  46.4 us (18%)
  local copies, waits for them, and re-layouts  34.6 us (13%)
  other arithmetic  23.6 us (9%)
    pallas_call x4, Pallas kernels, tensor_sum(): pl.pallas_call(reduce_kernel, out_shape=jax.ShapeDtypeStruct(part.shape,...  63.5 us
    pallas_call x1, Pallas kernels, ring_scatter(): pl.pallas_call(scatter_kernel, out_shape=(jax.ShapeDtypeStruct((rows, col...  46.4 us
    pallas_call x1, Pallas kernels, ring_gather(): pl.pallas_call(gather_kernel, out_shape=jax.ShapeDtypeStruct((rows * RING...  42.7 us
    unnamed x112, local copies, waits for them, and re-layouts  19.5 us
    dot_general x4, matrix products, times_transposed(): lax.dot_general(left_op, right_op, (((1,), (1,)), ((), ())), preferred_el...  10.2 us
    dot_general x4, matrix products, matmul(): return jnp.dot(left_op, right_op, preferred_element_type=jnp.float32)  8.86 us
    dot_general x1, matrix products, attend_backward(): jnp.einsum('hqk,qhe->khe', grad_scores, query_heads, preferred_element_ty...  7.53 us
    dot_general x1, matrix products, attend_backward(): jnp.einsum('hqk,khe->qhe', grad_scores, key_heads, preferred_element_type...  7.47 us

profile of v1, /device:TPU:0, one launch (start us, length us, event | category | flops | bytes accessed | tf_op | source)
XLA Modules:
  0.0 259.3 jit_solution(97263365935777364)
XLA Ops:
  12.8 42.7 %shard_map.218 = bf16[768,2304]{1,0:T(8,128)(2,1)} custom-call(bf16[96,2304]{1,0:T(8,128)(2,1)} %concatenate.36.share_ref), custom_call_target="tpu_custom_call" | custom-call | tf_op jit(solution)/shard_map/pallas_call | solution.py:104
  55.5 2.0 convolution_bitcast_fusion
  61.0 2.5 convolution_convert_fusion.6.part_ref
  63.5 15.8 %shard_map.219 = bf16[512,768]{1,0:T(8,128)(2,1)} custom-call(bf16[512,768]{1,0:T(8,128)(2,1)} %convolution_convert_fusion.6.part_ref), custom_call_target="tpu_custom_call" | custom-call | tf_op jit(solution)/shard_map/pallas_call | solution.py:276
  81.4 3.6 %multiply_convert_fusion.1 = (bf16[512,768]{1,0:T(8,128)(2,1)S(1)}, f32[512,768]{1,0:T(8,128)}) fusion(f32[768]{0:T(1024)S(1)} %add.201, bf16[768,2304]{1,0:T(8,128)(2,1)} %shard_map.218, f32[768]{0:T(1024)S(1)} %get-tuple-element.108, f32[768]{0:T(1024)S(1)} %get-tuple-element.109, f32[512]{0:T(512)S(1)} %add_rsqrt_fusion.1, ...), kind=kOutput, calls=%fused_computation.35 | convolution fusion | flops 609878016 | bytes 5128192 | tf_op jit(solution)/shard_map/dot_general | solution.py:307
  85.8 3.0 %convolution_convert_fusion.4.part_ref = bf16[512,768]{1,0:T(8,128)(2,1)} fusion(bf16[512,768]{1,0:T(8,128)(2,1)S(1)} %get-tuple-element.169, bf16[768,2304]{1,0:T(8,128)(2,1)} %shard_map.218), kind=kOutput, calls=%fused_computation.50 | convolution fusion | flops 604372992 | bytes 2752512 | tf_op jit(solution)/shard_map/dot_general | solution.py:317
  88.8 15.9 %shard_map.220 = bf16[512,768]{1,0:T(8,128)(2,1)} custom-call(bf16[512,768]{1,0:T(8,128)(2,1)} %convolution_convert_fusion.4.part_ref), custom_call_target="tpu_custom_call" | custom-call | tf_op jit(solution)/shard_map/pallas_call | solution.py:276
  104.7 1.9 fusion.92
  112.8 1.9 convolution_convert_fusion
  116.4 16.0 %shard_map.221 = bf16[512,768]{1,0:T(8,128)(2,1)} custom-call(bf16[512,768]{1,0:T(8,128)(2,1)} %convolution_convert_fusion.3.part_ref), custom_call_target="tpu_custom_call" | custom-call | tf_op jit(solution)/shard_map/pallas_call | solution.py:276
  132.4 2.2 multiply_reduce_fusion.1
  134.7 1.9 fusion.91
  136.6 2.1 convolution_convert_fusion.1
  141.5 3.5 %fusion.94 = (f32[3,64]{1,0:T(4,128)S(1)}, bf16[512,3,64]{0,2,1:T(8,128)(2,1)}) fusion(bf16[512,3,64]{0,2,1:T(8,128)(2,1)S(1)} %bitcast.214, f32[3,512]{1,0:T(4,128)S(1)} %log_add_fusion, f32[3,512,512]{1,2,0:T(8,128)} %copy-done.3, pred[512]{0:T(512)(128)(4,1)S(1)} %copy-done.36), kind=kOutput, calls=%fused_computation.195 | convolution fusion | flops 104005440 | bytes 3546368 | tf_op jit(solution)/shard_map/while/body/eval_jaxpr/hqk,qhe->khe/dot_general | solution.py:390
  145.7 2.3 fusion.102
  148.0 7.5 %fusion.33 = bf16[3,64,512]{2,1,0:T(8,128)(2,1)} fusion(bf16[512,3,64]{0,2,1:T(8,128)(2,1)S(1)} %bitcast.217, f32[3,512,512]{1,2,0:T(8,128)} %fusion.102, f32[3,512,512]{1,2,0:T(8,128)} %copy-done.3, f32[3,512]{1,0:T(4,128)S(1)} %log_add_fusion, pred[512]{0:T(512)(128)(4,1)} %copy-done.35), kind=kOutput, calls=%fused_computation.60 | convolution fusion | flops 109414400 | bytes 6691328 | tf_op jit(solution)/shard_map/while/body/eval_jaxpr/hqk,qhe->khe/dot_general | solution.py:387
  155.5 7.5 %fusion.95 = (f32[3,64]{1,0:T(4,128)S(1)}, bf16[512,3,64]{0,2,1:T(8,128)(2,1)}) fusion(bf16[512,3,64]{0,2,1:T(8,128)(2,1)S(1)} %bitcast.219, f32[3,512,512]{1,2,0:T(8,128)} %fusion.102, f32[3,512]{1,0:T(4,128)S(1)} %log_add_fusion, f32[3,512,512]{1,2,0:T(8,128)} %copy-done.3, pred[512]{0:T(512)(128)(4,1)S(1)} %copy-done.37), kind=kOutput, calls=%fused_computation.196 | convolution fusion | flops 109512512 | bytes 6692096 | tf_op jit(solution)/shard_map/while/body/eval_jaxpr/hqk,khe->qhe/dot_general | solution.py:384
  163.1 3.0 %convolution_convert_fusion.5.part_ref = bf16[512,768]{1,0:T(8,128)(2,1)} fusion(bf16[768,2304]{1,0:T(8,128)(2,1)} %shard_map.218, bf16[512,192]{0,1:T(8,128)(2,1)S(1)} %bitcast.224, bf16[512,192]{0,1:T(8,128)(2,1)S(1)} %bitcast.226, bf16[512,192]{0,1:T(8,128)(2,1)} %bitcast.228), kind=kOutput, calls=%fused_computation.51 | convolution fusion | flops 455147520 | bytes 2359296 | tf_op jit(solution)/shard_map/dot_general | solution.py:317
  166.1 15.8 %shard_map.222 = bf16[512,768]{1,0:T(8,128)(2,1)} custom-call(bf16[512,768]{1,0:T(8,128)(2,1)} %convolution_convert_fusion.5.part_ref), custom_call_target="tpu_custom_call" | custom-call | tf_op jit(solution)/shard_map/pallas_call | solution.py:276
  182.0 2.2 fusion.43
  186.9 6.0 %concatenate.38.grad_ref = bf16[768,2304]{1,0:T(8,128)(2,1)} concatenate(bf16[768,576]{1,0:T(8,128)(2,1)S(1)} %bitcast.210, bf16[768,192]{1,0:T(8,128)(2,1)S(1)} %copy.55, bf16[768,768]{1,0:T(8,128)(2,1)} %convolution_convert_fusion.1, bf16[768,768]{1,0:T(8,128)(2,1)S(1)} %copy-done.7), dimensions={1} | concatenate | bytes 7077888 | tf_op jit(solution)/shard_map/concatenate | solution.py:488
  192.9 46.4 %shard_map.223 = (f32[96,2304]{1,0:T(8,128)}, f32[8,1024]{1,0:T(8,128)}) custom-call(bf16[768,2304]{1,0:T(8,128)(2,1)} %concatenate.38.grad_ref, f32[8,1024]{1,0:T(8,128)} %select_maximum_fusion.small_ref), custom_call_target="tpu_custom_call" | custom-call | tf_op jit(solution)/shard_map/pallas_call | solution.py:198
  252.4 2.0 copy.65
  255.4 2.5 multiply_subtract_fusion
  (173 shorter events, 47.0 us)
Async XLA Ops:
  2.1 57.2 %copy-start.35 = (pred[512]{0:T(512)(128)(4,1)}, pred[512]{0:T(512)(128)(4,1)S(1)}, u32[]{:S(2)}) copy-start(pred[512]{0:T(512)(128)(4,1)S(1)} %get-tuple-element.182) | copy-start | bytes 1540
  12.8 42.7 %copy-start.1 = (bf16[1,512,768]{2,1,0:T(8,128)(2,1)S(1)}, bf16[1,512,768]{2,1,0:T(8,128)(2,1)}, u32[]{:S(2)}) copy-start(bf16[1,512,768]{2,1,0:T(8,128)(2,1)} %param.11) | copy-start | bytes 2359300
  107.8 2.5 copy-start.45
  108.7 2.4 copy-start.4
  136.6 2.7 %copy-start.2 = (f32[512,768]{1,0:T(8,128)S(1)}, f32[512,768]{1,0:T(8,128)}, u32[]{:S(2)}) copy-start(f32[512,768]{1,0:T(8,128)} %get-tuple-element.117) | copy-start | bytes 4718596
  141.5 4.2 %copy-start.22 = (bf16[512,192]{0,1:T(8,128)(2,1)S(1)}, bf16[512,192]{0,1:T(8,128)(2,1)}, u32[]{:S(2)}) copy-start(bf16[512,192]{0,1:T(8,128)(2,1)} %copy-done.21) | copy-start | bytes 589828
  148.0 7.5 %copy-start.26 = (bf16[512,192]{0,1:T(8,128)(2,1)S(1)}, bf16[512,192]{0,1:T(8,128)(2,1)}, u32[]{:S(2)}) copy-start(bf16[512,192]{0,1:T(8,128)(2,1)} %copy-done.25) | copy-start | bytes 589828
  148.0 7.5 %copy-start.37 = (pred[512]{0:T(512)(128)(4,1)S(1)}, pred[512]{0:T(512)(128)(4,1)}, u32[]{:S(2)}) copy-start(pred[512]{0:T(512)(128)(4,1)} %copy-done.35) | copy-start | bytes 1540
  155.5 7.6 %copy-start.40 = (bf16[512,3,64]{0,2,1:T(8,128)(2,1)S(1)}, bf16[512,3,64]{0,2,1:T(8,128)(2,1)}, u32[]{:S(2)}) copy-start(bf16[512,3,64]{0,2,1:T(8,128)(2,1)} %get-tuple-element.142) | copy-start | bytes 589828
  155.5 7.6 %copy-start.41 = (bf16[3,64,512]{2,1,0:T(8,128)(2,1)S(1)}, bf16[3,64,512]{2,1,0:T(8,128)(2,1)}, u32[]{:S(2)}) copy-start(bf16[3,64,512]{2,1,0:T(8,128)(2,1)} %fusion.33) | copy-start | bytes 589828
  182.0 3.0 %copy-start.42 = (bf16[512,3,64]{0,2,1:T(8,128)(2,1)S(1)}, bf16[512,3,64]{0,2,1:T(8,128)(2,1)}, u32[]{:S(2)}) copy-start(bf16[512,3,64]{0,2,1:T(8,128)(2,1)} %get-tuple-element.144) | copy-start | bytes 589828
  192.9 47.3 %copy-start.33 = (f32[6,192]{1,0:T(8,128)S(1)}, f32[6,192]{1,0:T(8,128)}, u32[]{:S(2)}) copy-start(f32[6,192]{1,0:T(8,128)} %param.16) | copy-start | bytes 13828
  192.9 47.3 %copy-start.34 = (f32[1,6,192]{2,0,1:T(1,128)S(1)}, f32[1,6,192]{2,0,1:T(1,128)}, u32[]{:S(2)}) copy-start(f32[1,6,192]{2,0,1:T(1,128)} %get-tuple-element.163) | copy-start | bytes 13828
  192.9 48.5 %copy-start.27 = (f32[1,6,768]{2,0,1:T(1,128)S(1)}, f32[1,6,768]{2,0,1:T(1,128)}, u32[]{:S(2)}) copy-start(f32[1,6,768]{2,0,1:T(1,128)} %get-tuple-element.160) | copy-start | bytes 55300
  192.9 49.2 %copy-start.30 = (f32[6,768]{1,0:T(8,128)S(1)}, f32[6,768]{1,0:T(8,128)}, u32[]{:S(2)}) copy-start(f32[6,768]{1,0:T(8,128)} %param.17) | copy-start | bytes 55300
  192.9 49.2 %copy-start.31 = (f32[1,6,768]{2,0,1:T(1,128)S(1)}, f32[1,6,768]{2,0,1:T(1,128)}, u32[]{:S(2)}) copy-start(f32[1,6,768]{2,0,1:T(1,128)} %get-tuple-element.159) | copy-start | bytes 55300
  239.4 9.0 %copy-start.10 = (f32[96,2304]{1,0:T(8,128)S(1)}, f32[96,2304]{1,0:T(8,128)}, u32[]{:S(2)}) copy-start(f32[96,2304]{1,0:T(8,128)} %get-tuple-element.57) | copy-start | bytes 2654212
  240.1 8.6 %copy-start.32 = (f32[6,192]{1,0:T(8,128)}, f32[6,192]{1,0:T(8,128)S(1)}, u32[]{:S(2)}) copy-start(f32[6,192]{1,0:T(8,128)S(1)} %get-tuple-element.115) | copy-start | bytes 13828
  246.3 3.5 %copy-start.9 = (f32[5,192,96]{1,2,0:T(8,128)S(1)}, f32[5,192,96]{1,2,0:T(8,128)}, u32[]{:S(2)}) copy-start(f32[5,192,96]{1,2,0:T(8,128)} %copy-done.8) | copy-start | bytes 1105924
  246.3 3.5 %copy-start.13 = (f32[1,5,192,96]{2,3,1,0:T(8,128)S(1)}, f32[1,5,192,96]{2,3,1,0:T(8,128)}, u32[]{:S(2)}) copy-start(f32[1,5,192,96]{2,3,1,0:T(8,128)} %copy.76) | copy-start | bytes 1105924
  246.3 3.5 %copy-start.14 = (f32[1,5,192,96]{2,3,1,0:T(8,128)S(1)}, f32[1,5,192,96]{2,3,1,0:T(8,128)}, u32[]{:S(2)}) copy-start(f32[1,5,192,96]{2,3,1,0:T(8,128)} %copy.75) | copy-start | bytes 1105924
  251.0 4.4 %copy-start.6 = (f32[2,7,96,192]{3,2,1,0:T(8,128)S(1)}, f32[2,7,96,192]{3,2,1,0:T(8,128)}, u32[]{:S(2)}) copy-start(f32[2,7,96,192]{3,2,1,0:T(8,128)} %param.18) | copy-start | bytes 3096580
  251.0 4.4 %copy-start.12 = (f32[7,96,192]{2,1,0:T(8,128)S(1)}, f32[7,96,192]{2,1,0:T(8,128)}, u32[]{:S(2)}) copy-start(f32[7,96,192]{2,1,0:T(8,128)} %param.14) | copy-start | bytes 1548292
  255.4 2.5 copy-start.17
  (22 other events, 34.2 us)

commit v2 on v1

--- a/solution.py
+++ b/solution.py
@@ -1,5 +1,3 @@
-import functools
-
 import jax
 import jax.numpy as jnp
 from jax import lax
@@ -45,17 +43,11 @@
     return me, place, (right, left)
 
 
-def greet(axis, devices):
-    barrier = pltpu.get_barrier_semaphore()
-    for device in devices:
-        pl.semaphore_signal(barrier, inc=1, device_id={axis: device}, device_id_type=MESH)
-    pl.semaphore_wait(barrier, len(devices))
-
-
 PIECES = 2
-
-
-def gather_kernel(share_ref, full_ref, local_sem, send_sem, recv_sem):
+PARTS = 4
+
+
+def gather_steps(share_ref, full_ref, local_sem, send_sem, recv_sem):
     me, place, targets = ring_neighbours()
     rows, columns = share_ref.shape
     piece_rows, half = rows // PIECES, columns // 2
@@ -67,7 +59,6 @@
     own_start = pl.multiple_of(me * rows, rows)
     own = pltpu.make_async_copy(share_ref, full_ref.at[pl.ds(own_start, rows)], local_sem)
     own.start()
-    greet("dp", targets)
     copies = {}
     for step in range(RING - 1):
         for piece in range(PIECES):
@@ -92,6 +83,7 @@
                 )
                 copy.start()
                 copies[step, piece, way] = copy
+        yield
     for (step, piece, way), copy in copies.items():
         copy.wait_send()
         if step == RING - 2:
@@ -99,46 +91,16 @@
     own.wait()
 
 
-def ring_gather(share):
-    rows, columns = share.shape
-    return pl.pallas_call(
-        gather_kernel,
-        out_shape=jax.ShapeDtypeStruct((rows * RING, columns), share.dtype),
-        in_specs=[pl.BlockSpec(memory_space=pltpu.VMEM)],
-        out_specs=pl.BlockSpec(memory_space=pltpu.VMEM),
-        scratch_shapes=[
-            pltpu.SemaphoreType.DMA,
-            pltpu.SemaphoreType.DMA((RING - 1, PIECES, 2)),
-            pltpu.SemaphoreType.DMA((RING - 1, PIECES, 2)),
-        ],
-        compiler_params=pltpu.CompilerParams(collective_id=0, has_side_effects=True),
-    )(share)
-
-
-def scatter_kernel(
-    grad_ref,
-    small_ref,
-    share_ref,
-    small_out_ref,
-    arrived,
-    leaving,
-    small_slots,
-    send_sem,
-    recv_sem,
-    small_send,
-    small_recv,
-):
+def scatter_steps(grad_ref, share_ref, arrived, leaving, send_sem, recv_sem):
     me, place, targets = ring_neighbours()
     rows, columns = share_ref.shape
     piece_rows, half = rows // PIECES, columns // 2
-    greet("dp", [(me + shift) % RING for shift in range(1, RING)])
 
     def grad_at(owner, piece, way):
         start = pl.multiple_of(owner * rows + piece * piece_rows, piece_rows)
         return grad_ref.at[pl.ds(start, piece_rows), pl.ds(way * half, half)]
 
     copies = {}
-    small_copies = []
     for step in range(RING - 1):
         for piece in range(PIECES):
             for way in range(2):
@@ -160,24 +122,33 @@
                 )
                 copy.start()
                 copies[step, piece, way] = copy
-        if step == 0:
-            for shift in range(1, RING):
-                copy = pltpu.make_async_remote_copy(
-                    src_ref=small_ref,
-                    dst_ref=small_slots.at[me],
-                    send_sem=small_send.at[shift - 1],
-                    recv_sem=small_recv.at[shift - 1],
-                    device_id={"dp": (me + shift) % RING},
-                    device_id_type=MESH,
-                )
-                copy.start()
-                small_copies.append(copy)
+        yield
     for piece in range(PIECES):
         for way in range(2):
             copies[RING - 2, piece, way].wait_recv()
             total = arrived[RING - 2, piece, way].astype(jnp.float32)
             total += grad_at(me, piece, way)[...].astype(jnp.float32)
             share_ref[pl.ds(piece * piece_rows, piece_rows), pl.ds(way * half, half)] = total
+    for copy in copies.values():
+        copy.wait_send()
+
+
+def small_steps(small_ref, small_out_ref, small_slots, small_send, small_recv):
+    me = lax.axis_index("dp")
+    small_copies = []
+    for shift in range(1, RING):
+        copy = pltpu.make_async_remote_copy(
+            src_ref=small_ref,
+            dst_ref=small_slots.at[me],
+            send_sem=small_send.at[shift - 1],
+            recv_sem=small_recv.at[shift - 1],
+            device_id={"dp": (me + shift) % RING},
+            device_id_type=MESH,
+        )
+        copy.start()
+        small_copies.append(copy)
+    for turn in range(4):
+        yield
     for copy in small_copies:
         copy.wait_recv()
     small_slots[me] = small_ref[...]
@@ -187,46 +158,18 @@
     small_out_ref[...] = small_total
     for copy in small_copies:
         copy.wait_send()
-    for copy in copies.values():
-        copy.wait_send()
-
-
-def ring_scatter(grads, small):
-    rows, columns = grads.shape[0] // RING, grads.shape[1]
-    slot_shape = (RING - 1, PIECES, 2, rows // PIECES, columns // 2)
-    vmem = pl.BlockSpec(memory_space=pltpu.VMEM)
-    return pl.pallas_call(
-        scatter_kernel,
-        out_shape=(
-            jax.ShapeDtypeStruct((rows, columns), jnp.float32),
-            jax.ShapeDtypeStruct(small.shape, jnp.float32),
-        ),
-        in_specs=[vmem, vmem],
-        out_specs=(vmem, vmem),
-        scratch_shapes=[
-            pltpu.VMEM(slot_shape, jnp.bfloat16),
-            pltpu.VMEM(slot_shape, jnp.bfloat16),
-            pltpu.VMEM((RING,) + small.shape, jnp.float32),
-            pltpu.SemaphoreType.DMA(slot_shape[:3]),
-            pltpu.SemaphoreType.DMA(slot_shape[:3]),
-            pltpu.SemaphoreType.DMA((RING - 1,)),
-            pltpu.SemaphoreType.DMA((RING - 1,)),
-        ],
-        compiler_params=pltpu.CompilerParams(collective_id=1, has_side_effects=True),
-    )(grads, small)
-
-
-PARTS = 4
-
-
-def reduce_kernel(part_ref, sum_ref, near, chip_sum, far, total, send_sem, recv_sem):
+
+
+def tensor_partners():
     me = lax.axis_index("tensor")
-    core = me % 2
-    partner = me + 1 - 2 * core
-    across = (me + 2) % 4
+    return me + 1 - 2 * (me % 2), (me + 2) % 4
+
+
+def sum_steps(part_ref, sum_ref, near, chip_sum, far, total, send_sem, recv_sem):
+    core = lax.axis_index("tensor") % 2
+    partner, across = tensor_partners()
     half = part_ref.shape[0] // 2
     size = half // PARTS
-    greet("tensor", (partner, across))
 
     def rows_of(side, piece):
         return pl.ds(pl.multiple_of(side * half + piece * size, size), size)
@@ -253,12 +196,15 @@
         chip = near[piece].astype(jnp.float32) + part_ref[rows_of(core, piece)].astype(jnp.float32)
         chip_sum[piece] = chip.astype(jnp.bfloat16)
         second.append(send(chip_sum.at[piece], far.at[piece], 1, piece, across))
+    yield
     third = []
     for piece in range(PARTS):
         second[piece].wait_recv()
         both = chip_sum[piece].astype(jnp.float32) + far[piece].astype(jnp.float32)
         total[piece] = both.astype(jnp.bfloat16)
         third.append(send(total.at[piece], sum_ref.at[rows_of(core, piece)], 2, piece, partner))
+        if piece % 2:
+            yield
     for piece in range(PARTS):
         third[piece].wait_recv()
         sum_ref[rows_of(core, piece)] = total[piece]
@@ -266,41 +212,188 @@
         copy.wait_send()
 
 
-def tensor_sum(part, call):
-    part = part.astype(jnp.bfloat16)
-    if lax.axis_size("tensor") != 4 or part.shape[0] % 128:
-        return lax.psum(part, "tensor").astype(jnp.float32)
-    rows, columns = part.shape
+def take_turns(*plans):
+    plans = list(plans)
+    while plans:
+        for plan in list(plans):
+            if next(plan, "done") == "done":
+                plans.remove(plan)
+
+
+def greet_all(ring=(), tensor=()):
+    barrier = pltpu.get_barrier_semaphore()
+    for axis, devices in (("dp", ring), ("tensor", tensor)):
+        for device in devices:
+            pl.semaphore_signal(barrier, inc=1, device_id={axis: device}, device_id_type=MESH)
+    pl.semaphore_wait(barrier, len(ring) + len(tensor))
+
+
+def first_gather_kernel(in_ref, out_ref, full_ref, rest_ref, wide, share, *sems):
+    width = in_ref.shape[2]
+    for index in range(12):
+        if index == 3 or index >= 8:
+            block = out_ref[0 if index == 3 else index - 7].T
+        else:
+            block = in_ref[index if index < 3 else index - 1]
+        wide[:, index * width : (index + 1) * width] = block
+    share[...] = wide[:, : 4 * width].astype(jnp.bfloat16)
+    rest_ref[...] = wide[:, 4 * width :].astype(jnp.bfloat16)
+    greet_all(ring_neighbours()[2])
+    take_turns(gather_steps(share, full_ref, *sems))
+
+
+def second_gather_kernel(share_ref, part_ref, full_ref, sum_ref, *scratch):
+    greet_all(ring_neighbours()[2], tensor_partners())
+    take_turns(
+        gather_steps(share_ref, full_ref, *scratch[:3]), sum_steps(part_ref, sum_ref, *scratch[3:])
+    )
+
+
+def sum_kernel(part_ref, sum_ref, *scratch):
+    greet_all((), tensor_partners())
+    take_turns(sum_steps(part_ref, sum_ref, *scratch))
+
+
+def first_scatter_kernel(grad_ref, part_ref, share_ref, sum_ref, *scratch):
+    greet_all(ring_neighbours()[2], tensor_partners())
+    take_turns(
+        scatter_steps(grad_ref, share_ref, *scratch[:4]),
+        sum_steps(part_ref, sum_ref, *scratch[4:]),
+    )
+
+
+def second_scatter_kernel(
+    grad_ref, part_ref, small_ref, share_ref, sum_ref, small_out_ref, *scratch
+):
+    me = lax.axis_index("dp")
+    greet_all([(me + shift) % RING for shift in range(1, RING)], tensor_partners())
+    take_turns(
+        scatter_steps(grad_ref, share_ref, *scratch[:4]),
+        sum_steps(part_ref, sum_ref, *scratch[4:10]),
+        small_steps(small_ref, small_out_ref, *scratch[10:]),
+    )
+
+
+def gather_scratch():
+    shape = (RING - 1, PIECES, 2)
+    return [pltpu.SemaphoreType.DMA, pltpu.SemaphoreType.DMA(shape), pltpu.SemaphoreType.DMA(shape)]
+
+
+def scatter_scratch(rows, columns):
+    shape = (RING - 1, PIECES, 2)
+    slots = pltpu.VMEM(shape + (rows // PIECES, columns // 2), jnp.bfloat16)
+    return [slots, slots, pltpu.SemaphoreType.DMA(shape), pltpu.SemaphoreType.DMA(shape)]
+
+
+def small_scratch(small):
+    sems = pltpu.SemaphoreType.DMA((RING - 1,))
+    return [pltpu.VMEM((RING,) + small.shape, jnp.float32), sems, sems]
+
+
+def sum_scratch(rows, columns):
     slots = pltpu.VMEM((PARTS, rows // (2 * PARTS), columns), jnp.bfloat16)
+    sems = pltpu.SemaphoreType.DMA((3, PARTS))
+    return [slots, slots, slots, slots, sems, sems]
+
+
+def kernel_call(kernel, operands, results, scratch, collective_id):
     vmem = pl.BlockSpec(memory_space=pltpu.VMEM)
+    extra = {} if collective_id is None else {"collective_id": collective_id, "has_side_effects": True}
     return pl.pallas_call(
-        reduce_kernel,
-        out_shape=jax.ShapeDtypeStruct(part.shape, jnp.bfloat16),
-        in_specs=[vmem],
-        out_specs=vmem,
-        scratch_shapes=[
-            slots,
-            slots,
-            slots,
-            slots,
-            pltpu.SemaphoreType.DMA((3, PARTS)),
-            pltpu.SemaphoreType.DMA((3, PARTS)),
-        ],
-        compiler_params=pltpu.CompilerParams(collective_id=2 + call, has_side_effects=True),
-    )(part).astype(jnp.float32)
-
-
-def gather_weights(share):
-    if lax.axis_size("dp") == RING and share.shape[0] % 32 == 0:
-        return ring_gather(share)
-    return lax.all_gather(share, "dp", axis=0, tiled=True)
-
-
-def scatter_grads(grads, small):
-    if lax.axis_size("dp") == RING and grads.shape[0] % (32 * RING) == 0:
-        return ring_scatter(grads, small)
+        kernel,
+        out_shape=tuple(jax.ShapeDtypeStruct(shape, dtype) for shape, dtype in results),
+        in_specs=[vmem] * len(operands),
+        out_specs=(vmem,) * len(results),
+        scratch_shapes=scratch,
+        compiler_params=pltpu.CompilerParams(**extra),
+    )(*operands)
+
+
+def ring_here(rows):
+    return (
+        lax.axis_size("dp") == RING
+        and lax.axis_size("tensor") == 4
+        and rows % 32 == 0
+    )
+
+
+def gather_first(in_weight, out_weight):
+    rows, group_width = in_weight.shape[1:]
+    if ring_here(rows):
+        return kernel_call(
+            first_gather_kernel,
+            (in_weight, out_weight),
+            [
+                ((RING * rows, 4 * group_width), jnp.bfloat16),
+                ((rows, 8 * group_width), jnp.bfloat16),
+            ],
+            [
+                pltpu.VMEM((rows, 12 * group_width), jnp.float32),
+                pltpu.VMEM((rows, 4 * group_width), jnp.bfloat16),
+            ]
+            + gather_scratch(),
+            0,
+        )
+    in_low = in_weight.astype(jnp.bfloat16)
+    out_low = out_weight.astype(jnp.bfloat16).swapaxes(1, 2)
+    share = jnp.concatenate(list(in_low[:3]) + [out_low[0]], 1)
+    rest = jnp.concatenate(list(in_low[3:]) + list(out_low[1:]), 1)
+    return lax.all_gather(share, "dp", axis=0, tiled=True), rest
+
+
+def plain_sum(part):
+    if lax.axis_size("tensor") == 4 and part.shape[0] % 128 == 0:
+        results = [(part.shape, jnp.bfloat16)]
+        return kernel_call(sum_kernel, (part,), results, sum_scratch(*part.shape), 1)[0]
+    return lax.psum(part, "tensor")
+
+
+def gather_second(rest, part):
+    rows, columns = rest.shape
+    if ring_here(rows):
+        return kernel_call(
+            second_gather_kernel,
+            (rest, part),
+            [((RING * rows, columns), jnp.bfloat16), (part.shape, jnp.bfloat16)],
+            gather_scratch() + sum_scratch(*part.shape),
+            2,
+        )
+    return lax.all_gather(rest, "dp", axis=0, tiled=True), lax.psum(part, "tensor")
+
+
+def scatter_plain(grads):
     share = lax.psum_scatter(grads, "dp", scatter_dimension=0, tiled=True)
-    return share.astype(jnp.float32), lax.psum(small, "dp")
+    return share.astype(jnp.float32)
+
+
+def scatter_first(grads, part):
+    rows, columns = grads.shape[0] // lax.axis_size("dp"), grads.shape[1]
+    if ring_here(rows):
+        return kernel_call(
+            first_scatter_kernel,
+            (grads, part),
+            [((rows, columns), jnp.float32), (part.shape, jnp.bfloat16)],
+            scatter_scratch(rows, columns) + sum_scratch(*part.shape),
+            3,
+        )
+    return scatter_plain(grads), lax.psum(part, "tensor")
+
+
+def scatter_second(grads, part, small):
+    rows, columns = grads.shape[0] // lax.axis_size("dp"), grads.shape[1]
+    if ring_here(rows):
+        return kernel_call(
+            second_scatter_kernel,
+            (grads, part, small),
+            [
+                ((rows, columns), jnp.float32),
+                (part.shape, jnp.bfloat16),
+                (small.shape, jnp.float32),
+            ],
+            scatter_scratch(rows, columns) + sum_scratch(*part.shape) + small_scratch(small),
+            4,
+        )
+    return scatter_plain(grads), lax.psum(part, "tensor"), lax.psum(small, "dp")
 
 
 def matmul(left_op, right_op):
@@ -400,6 +493,65 @@
     second_hat = second / (1.0 - beta_second**step_count)
     new_param = param - learn_rate * (first_hat / (jnp.sqrt(second_hat) + adam_eps) + decay * param)
     return (new_param, jnp.stack([first, second]))
+
+
+def adam_store(param, grad, moments, decay, new_param, new_moments):
+    first = beta_first * moments[0] + (1.0 - beta_first) * grad
+    second = beta_second * moments[1] + (1.0 - beta_second) * grad * grad
+    first_hat = first / (1.0 - beta_first**step_count)
+    second_hat = second / (1.0 - beta_second**step_count)
+    step = first_hat / (jnp.sqrt(second_hat) + adam_eps) + decay * param
+    new_param[...] = param - learn_rate * step
+    new_moments[0] = first
+    new_moments[1] = second
+
+
+def adam_kernel(share_ref, rest_ref, small_ref, *refs):
+    params, moments = refs[:4], refs[4:8]
+    grads, new_params, new_moments = refs[8:12], refs[12:16], refs[16:20]
+    matrix_in, matrix_out = params[0], params[1]
+    width = matrix_in.shape[2]
+    for index in range(12):
+        source, place = (share_ref, index) if index < 4 else (rest_ref, index - 4)
+        grad = source[:, place * width : (place + 1) * width]
+        if index == 3 or index >= 8:
+            group, spot, grad = 1, (0 if index == 3 else index - 7), grad.T
+        else:
+            group, spot = 0, (index if index < 3 else index - 1)
+        grads[group][spot] = grad
+        adam_store(
+            params[group][spot],
+            grad,
+            (moments[group][0, spot], moments[group][1, spot]),
+            weight_decay,
+            new_params[group].at[spot],
+            new_moments[group].at[:, spot],
+        )
+    model_width = params[3].shape[1]
+    for group, start in ((2, model_width), (3, 0)):
+        grad = small_ref[:6, start : start + params[group].shape[1]]
+        grads[group][...] = grad
+        adam_store(
+            params[group][...], grad, moments[group], 0.0, new_params[group], new_moments[group]
+        )
+
+
+def update_all(share, rest, small, params, moments):
+    group_width, width = params[0].shape[2], params[3].shape[1]
+    if ring_here(params[0].shape[1]):
+        shapes = [(a.shape, jnp.float32) for a in params + params + moments]
+        return kernel_call(adam_kernel, (share, rest, small) + params + moments, shapes, [], None)
+    total = jnp.concatenate([share, rest], 1)
+    blocks = [total[:, k * group_width : (k + 1) * group_width] for k in range(12)]
+    grads = (
+        jnp.stack(blocks[:3] + blocks[4:8]),
+        jnp.stack([blocks[3]] + blocks[8:]).swapaxes(1, 2),
+        small[:6, width : width + group_width],
+        small[:6, :width],
+    )
+    decays = (weight_decay, weight_decay, 0.0, 0.0)
+    news = [adam_update(*group) for group in zip(params, grads, moments, decays)]
+    return grads + tuple(n[0] for n in news) + tuple(n[1] for n in news)
 
 
 def local(
@@ -417,16 +569,11 @@
 ):
     seq_count, seq_len, width = tokens.shape
     row_count = seq_count * seq_len
-    in_low = in_weight.astype(jnp.bfloat16)
-    out_low = out_weight.astype(jnp.bfloat16).swapaxes(1, 2)
-    share = jnp.concatenate(list(in_low[:3]) + [out_low[0]] + list(in_low[3:]) + list(out_low[1:]), 1)
-    full = gather_weights(share)
+    first_full, rest = gather_first(in_weight, out_weight)
     group_width = in_weight.shape[2]
     heads_here = group_width // HDIM
-    w_qkv = full[:, : 3 * group_width]
-    w_proj = full[:, 3 * group_width : 4 * group_width]
-    w_up = full[:, 4 * group_width : 8 * group_width]
-    w_down = full[:, 8 * group_width :]
+    w_qkv = first_full[:, : 3 * group_width]
+    w_proj = first_full[:, 3 * group_width :]
     bias_up = in_bias[2:6].reshape(1, 4 * group_width)
 
     def split_heads(flat_rows):
@@ -442,14 +589,18 @@
         (split_heads(query), split_heads(keys_low), split_heads(values_low), lengths),
     )
     mixed_flat = mixed_heads.reshape(row_count, group_width)
-    attn_out = tensor_sum(times_transposed(mixed_flat, w_proj), 0)
+    attn_part = times_transposed(mixed_flat, w_proj).astype(jnp.bfloat16)
+    second_full, attn_out = gather_second(rest, attn_part)
+    w_up = second_full[:, : 4 * group_width]
+    w_down = second_full[:, 4 * group_width :]
     hidden, normed_one, inverse_one = layer_norm(
-        flat_tokens.astype(jnp.float32) + attn_out + norm_vec[0], norm_vec[1], norm_vec[2]
+        flat_tokens.astype(jnp.float32) + attn_out.astype(jnp.float32) + norm_vec[0], norm_vec[1], norm_vec[2]
     )
     hidden_low = hidden.astype(jnp.bfloat16)
     pre_act = matmul(hidden_low, w_up) + bias_up
     act_low = gelu_value(pre_act).astype(jnp.bfloat16)
-    ffn_out = tensor_sum(times_transposed(act_low, w_down), 1)
+    ffn_part = times_transposed(act_low, w_down).astype(jnp.bfloat16)
+    ffn_out = plain_sum(ffn_part).astype(jnp.float32)
     out_rows, normed_two, inverse_two = layer_norm(
         hidden + ffn_out + norm_vec[3], norm_vec[4], norm_vec[5]
     )
@@ -463,7 +614,10 @@
     grad_pre = grad_act * gelu_slope(pre_act)
     grad_pre_low = grad_pre.astype(jnp.bfloat16)
     grad_up = inner_rows(hidden_low, grad_pre_low).astype(jnp.bfloat16)
-    grad_hidden = grad_two + tensor_sum(times_transposed(grad_pre_low, w_up), 2)
+    rest_grads = jnp.concatenate([grad_up, grad_down], 1)
+    back_part = times_transposed(grad_pre_low, w_up).astype(jnp.bfloat16)
+    rest_total, back_sum = scatter_first(rest_grads, back_part)
+    grad_hidden = grad_two + back_sum.astype(jnp.float32)
     grad_one = norm_back(grad_hidden, normed_one, inverse_one, norm_vec[1])
     grad_one_low = grad_one.astype(jnp.bfloat16)
     grad_proj = inner_rows(grad_one_low, mixed_flat).astype(jnp.bfloat16)
@@ -483,9 +637,9 @@
     grad_keys = grad_keys.reshape(row_count, group_width)
     grad_values = grad_values.reshape(row_count, group_width)
     qkv_grad_low = jnp.concatenate([grad_query, grad_keys, grad_values], 1).astype(jnp.bfloat16)
-    grad_input = grad_one + tensor_sum(times_transposed(qkv_grad_low, w_qkv), 3)
+    input_part = times_transposed(qkv_grad_low, w_qkv).astype(jnp.bfloat16)
     grad_qkv = inner_rows(flat_tokens, qkv_grad_low).astype(jnp.bfloat16)
-    grads = jnp.concatenate([grad_qkv, grad_proj, grad_up, grad_down], 1)
+    first_grads = jnp.concatenate([grad_qkv, grad_proj], 1)
     bias_rows = jnp.concatenate(
         [jnp.sum(grad_query, 0), jnp.sum(grad_values, 0), jnp.sum(grad_pre, 0)]
     ).reshape(6, group_width)
@@ -500,34 +654,17 @@
         ]
     )
     small = jnp.pad(jnp.concatenate([norm_rows, bias_rows], 1), ((0, 2), (0, 64)))
-    share_total, small_total = scatter_grads(grads, small)
-    norm_total = small_total[:6, :width]
-    bias_total = small_total[:6, width : width + group_width]
-    blocks = [share_total[:, k * group_width : (k + 1) * group_width] for k in range(12)]
-    in_share = jnp.stack(blocks[:3] + blocks[4:8])
-    out_share = jnp.stack([blocks[3]] + blocks[8:]).swapaxes(1, 2)
-    new_in_weight, new_in_moments = adam_update(in_weight, in_share, in_moments, weight_decay)
-    new_out_weight, new_out_moments = adam_update(out_weight, out_share, out_moments, weight_decay)
-    new_in_bias, new_bias_moments = adam_update(in_bias, bias_total, bias_moments, 0.0)
-    new_norm_vec, new_norm_moments = adam_update(norm_vec, norm_total, norm_moments, 0.0)
+    share_total, input_sum, small_total = scatter_second(first_grads, input_part, small)
+    grad_input = grad_one + input_sum.astype(jnp.float32)
+    params = (in_weight, out_weight, in_bias, norm_vec)
+    moments = (in_moments, out_moments, bias_moments, norm_moments)
+    updates = update_all(share_total, rest_total, small_total, params, moments)
     output = out_rows.astype(jnp.bfloat16).reshape(seq_count, seq_len, width)
     grad_tokens = grad_input.astype(jnp.bfloat16).reshape(seq_count, seq_len, width)
     return (
         output,
         grad_tokens,
-        in_share,
-        out_share,
-        bias_total,
-        norm_total,
-        new_in_weight,
-        new_out_weight,
-        new_in_bias,
-        new_norm_vec,
-        new_in_moments,
-        new_out_moments,
-        new_bias_moments,
-        new_norm_moments,
-    )
+    ) + tuple(updates)
 
 
 def solution(mesh):

time: 261 us -> 222 us (0.85)
  local copies, waits for them, and re-layouts: 34.6 us -> 10.4 us
  other arithmetic: 23.6 us -> 17.7 us
  matrix products: 46.4 us -> 41 us
  Pallas kernels: 153 us -> 150 us
    unnamed x112 -> x72, local copies, waits for them, and re-layouts: 19.5 us -> 7.42 us
    concatenate x2 -> x0, local copies, waits for them, and re-layouts: 6.97 us -> none  [the longest x1 6 us: local(): grads = jnp.concatenate([grad_qkv, grad_proj, grad_up, grad_down], 1)]
    another operation x9 -> x0, other arithmetic: 5.2 us -> none  [adam_update(): return (new_param, jnp.stack([first, second]))]
    slice x3 -> x0, local copies, waits for them, and re-layouts: 2.93 us -> none  [adam_update(): second = beta_second * moments[1] + (1.0 - beta_second) * grad * grad]
    concatenate x0 -> x2, other arithmetic: none -> 2.84 us  [the longest x1 1.62 us: local(): rest_grads = jnp.concatenate([grad_up, grad_down], 1)]
    dot_general x4, matrix products: 10.2 us -> 7.53 us  [times_transposed(): lax.dot_general(left_op, right_op, (((1,), (1,)), ((), ())), preferred_el...]
    pallas_call x6, Pallas kernels: 153 us -> 150 us  [kernel_call(): pl.pallas_call(kernel, out_shape=tuple((jax.ShapeDtypeStruct(shape, dtype...]
where the time goes in v2:
time: 222 us; the launch traced here: 221 us
  Pallas kernels  150 us (68%)
  matrix products  41 us (18%)
  other arithmetic  17.7 us (8%)
  local copies, waits for them, and re-layouts  10.4 us (5%)
    pallas_call x6, Pallas kernels, kernel_call(): pl.pallas_call(kernel, out_shape=tuple((jax.ShapeDtypeStruct(shape, dtype...  150 us
    dot_general x4, matrix products, matmul(): return jnp.dot(left_op, right_op, preferred_element_type=jnp.float32)  9.67 us
    dot_general x4, matrix products, times_transposed(): lax.dot_general(left_op, right_op, (((1,), (1,)), ((), ())), preferred_el...  7.53 us
    unnamed x72, local copies, waits for them, and re-layouts  7.42 us
    dot_general x1, matrix products, attend_backward(): jnp.einsum('hqk,qhe->khe', grad_scores, query_heads, preferred_element_ty...  6.64 us
    dot_general x1, matrix products, attend_backward(): jnp.einsum('hqk,khe->qhe', grad_scores, key_heads, preferred_element_type...  6.59 us

profile of v2, /device:TPU:0, one launch (start us, length us, event | category | flops | bytes accessed | tf_op | source)
XLA Modules:
  0.0 221.0 jit_solution(10537097024468459635)
XLA Ops:
  0.6 30.4 %shard_map.218 = (bf16[768,768]{1,0:T(8,128)(2,1)}, bf16[96,1536]{1,0:T(8,128)(2,1)}) custom-call(f32[7,96,192]{2,1,0:T(8,128)} %refs_0_.1, f32[5,192,96]{2,1,0:T(8,128)} %refs_1_.1), custom_call_target="tpu_custom_call" | custom-call | tf_op jit(solution)/shard_map/pallas_call | solution.py:302
  31.1 2.2 convolution_bitcast_fusion
  38.2 2.4 %convolution_convert_fusion.6.part_ref = bf16[512,768]{1,0:T(8,128)(2,1)} fusion(bf16[512,192]{0,1:T(8,128)(2,1)S(1)} %bitcast.83, bf16[768,768]{1,0:T(8,128)(2,1)} %get-tuple-element.87), kind=kOutput, calls=%fused_computation.53 | convolution fusion | flops 151388160 | bytes 1376256 | tf_op jit(solution)/shard_map/dot_general | solution.py:410
  40.6 34.0 %shard_map.219 = (bf16[768,1536]{1,0:T(8,128)(2,1)}, bf16[512,768]{1,0:T(8,128)(2,1)}) custom-call(bf16[96,1536]{1,0:T(8,128)(2,1)} %get-tuple-element.86.share_ref, bf16[512,768]{1,0:T(8,128)(2,1)} %convolution_convert_fusion.6.part_ref), custom_call_target="tpu_custom_call" | custom-call | tf_op jit(solution)/shard_map/pallas_call | solution.py:302
  77.3 3.7 %multiply_convert_fusion.1 = (bf16[512,768]{1,0:T(8,128)(2,1)S(1)}, f32[512,768]{1,0:T(8,128)}) fusion(f32[768]{0:T(1024)S(1)} %add.135, bf16[768,1536]{1,0:T(8,128)(2,1)} %get-tuple-element.89, f32[768]{0:T(1024)S(1)} %get-tuple-element.146, f32[768]{0:T(1024)S(1)} %get-tuple-element.147, f32[512]{0:T(512)S(1)} %add_rsqrt_fusion.1, ...), kind=kOutput, calls=%fused_computation.36 | convolution fusion | flops 609878016 | bytes 5128192 | tf_op jit(solution)/shard_map/dot_general | solution.py:400
  82.0 1.7 convolution_convert_fusion.4.part_ref
  83.6 14.9 %shard_map.220 = bf16[512,768]{1,0:T(8,128)(2,1)} custom-call(bf16[512,768]{1,0:T(8,128)(2,1)} %convolution_convert_fusion.4.part_ref), custom_call_target="tpu_custom_call" | custom-call | tf_op jit(solution)/shard_map/pallas_call | solution.py:302
  98.6 1.9 fusion.69
  103.1 2.4 %fusion.23 = (f32[512,768]{1,0:T(8,128)S(1)}, bf16[1,512,768]{2,1,0:T(8,128)(2,1)}) fusion(f32[512,768]{1,0:T(8,128)S(1)} %get-tuple-element.153, bf16[1,512,768]{2,1,0:T(8,128)(2,1)S(1)} %copy-done.5, f32[512]{0:T(512)S(1)} %broadcast_multiply_fusion.2, f32[512]{0:T(512)S(1)} %broadcast_multiply_fusion.3, f32[512]{0:T(512)} %copy-done.19, ...), kind=kLoop, calls=%fused_computation.25 | loop fusion | flops 4718592 | bytes 4734976 | tf_op jit(solution)/shard_map/mul | solution.py:425
  105.5 1.7 fusion.75
  107.2 1.7 convolution_convert_fusion.3.part_ref
  110.9 1.6 pad_maximum_fusion.grad_ref
  112.5 33.5 %shard_map.221 = (f32[96,1536]{1,0:T(8,128)}, bf16[512,768]{1,0:T(8,128)(2,1)}) custom-call(bf16[768,1536]{1,0:T(8,128)(2,1)} %pad_maximum_fusion.grad_ref, bf16[512,768]{1,0:T(8,128)(2,1)} %convolution_convert_fusion.3.part_ref), custom_call_target="tpu_custom_call" | custom-call | tf_op jit(solution)/shard_map/pallas_call | solution.py:302
  146.1 2.2 %multiply_reduce_fusion.1 = (f32[768]{0:T(1024)S(1)}, f32[512]{0:T(512)S(1)}, f32[512]{0:T(512)S(1)}, f32[768]{0:T(1024)S(1)}, f32[768]{0:T(1024)S(1)}) fusion(f32[512,768]{1,0:T(8,128)S(1)} %get-tuple-element.154, bf16[512,768]{1,0:T(8,128)(2,1)} %get-tuple-element.90, f32[512]{0:T(512)S(1)} %copy-done.17, f32[512]{0:T(512)S(1)} %broadcast_multiply_fusion.5, ...), kind=kLoop, calls=%fused_computation.29 | loop fusion | flops 6288128 | bytes 3955712 | tf_op jit(solution)/shard_map/reduce_sum | solution.py:649
  148.4 2.1 fusion.68
  150.6 2.0 convolution_convert_fusion.8
  152.7 2.3 %fusion.76 = f32[3,512,512]{1,2,0:T(8,128)} fusion(bf16[512,3,64]{0,2,1:T(8,128)(2,1)S(1)} %bitcast.77, bf16[512,3,64]{0,2,1:T(8,128)(2,1)S(1)} %bitcast.76), kind=kOutput, calls=%fused_computation.123 | convolution fusion | flops 100663296 | bytes 3538944 | tf_op jit(solution)/shard_map/while/body/eval_jaxpr/qhe,khe->hqk/dot_general | solution.py:472
  155.0 6.6 %fusion.71 = (f32[3,64]{1,0:T(4,128)S(1)}, bf16[512,3,64]{0,2,1:T(8,128)(2,1)S(1)}) fusion(bf16[512,3,64]{0,2,1:T(8,128)(2,1)S(1)} %bitcast.82, f32[3,512,512]{1,2,0:T(8,128)} %fusion.76, f32[3,512]{1,0:T(4,128)S(1)} %copy-done.27, f32[3,512,512]{1,2,0:T(8,128)} %copy-done.3, pred[512]{0:T(512)(128)(4,1)S(1)} %copy-done.29), kind=kOutput, calls=%fused_computation.120 | convolution fusion | flops 109512512 | bytes 6692096 | tf_op jit(solution)/shard_map/while/body/eval_jaxpr/hqk,khe->qhe/dot_general | solution.py:477
  161.7 2.9 %fusion.70 = (f32[3,64]{1,0:T(4,128)S(1)}, bf16[512,3,64]{0,2,1:T(8,128)(2,1)S(1)}) fusion(bf16[512,3,64]{0,2,1:T(8,128)(2,1)S(1)} %bitcast.78, f32[3,512]{1,0:T(4,128)S(1)} %copy-done.27, f32[3,512,512]{1,2,0:T(8,128)} %copy-done.3, pred[512]{0:T(512)(128)(4,1)S(1)} %copy-done.29), kind=kOutput, calls=%fused_computation.119 | convolution fusion | flops 104005440 | bytes 3546368 | tf_op jit(solution)/shard_map/while/body/eval_jaxpr/hqk,qhe->khe/dot_general | solution.py:483
  165.4 6.6 %fusion.33 = bf16[3,64,512]{2,1,0:T(8,128)(2,1)S(1)} fusion(bf16[512,3,64]{0,2,1:T(8,128)(2,1)S(1)} %bitcast.80, f32[3,512,512]{1,2,0:T(8,128)} %fusion.76, f32[3,512,512]{1,2,0:T(8,128)} %copy-done.3, f32[3,512]{1,0:T(4,128)S(1)} %copy-done.27, pred[512]{0:T(512)(128)(4,1)S(1)} %copy-done.29), kind=kOutput, calls=%fused_computation.61 | convolution fusion | flops 109414400 | bytes 6691328 | tf_op jit(solution)/shard_map/while/body/eval_jaxpr/hqk,qhe->khe/dot_general | solution.py:480
  172.1 1.7 convolution_convert_fusion.5.part_ref
  175.3 1.7 copy.43
  178.8 31.9 %shard_map.222 = (f32[96,768]{1,0:T(8,128)}, bf16[512,768]{1,0:T(8,128)(2,1)}, f32[8,1024]{1,0:T(8,128)}) custom-call(bf16[768,768]{1,0:T(8,128)(2,1)} %pad_maximum_fusion.1.grad_ref, bf16[512,768]{1,0:T(8,128)(2,1)} %convolution_convert_fusion.5.part_ref, f32[8,1024]{1,0:T(8,128)} %select_maximum_fusion.small_ref), custom_call_target="tpu_custom_call" | custom-call | tf_op jit(solution)/shard_map/pallas_call | solution.py:302
  211.9 5.3 %shard_map.223 = (f32[7,96,192]{2,1,0:T(8,128)}, f32[5,192,96]{2,1,0:T(8,128)}, f32[6,192]{1,0:T(8,128)}, f32[6,768]{1,0:T(8,128)}, f32[7,96,192]{2,1,0:T(8,128)...) custom-call(f32[96,768]{1,0:T(8,128)} %get-tuple-element.92.share_re, ...), custom_call_target="tpu_custom_call" | custom-call | tf_op jit(solution)/shard_map/pallas_call | solution.py:302
  (114 shorter events, 21.5 us)
Async XLA Ops:
  31.1 2.2 %copy-start.18 = (f32[6,192]{1,0:T(8,128)S(1)}, f32[6,192]{1,0:T(8,128)}, u32[]{:S(2)}) copy-start(f32[6,192]{1,0:T(8,128)} %refs_2_.1) | copy-start | bytes 13828
  34.2 66.7 %copy-start.19 = (f32[512]{0:T(512)}, f32[512]{0:T(512)S(1)}, u32[]{:S(2)}) copy-start(f32[512]{0:T(512)S(1)} %get-tuple-element.173) | copy-start | bytes 6148
  37.5 37.1 %copy-start.14 = (f32[6,768]{1,0:T(8,128)S(1)}, f32[6,768]{1,0:T(8,128)}, u32[]{:S(2)}) copy-start(f32[6,768]{1,0:T(8,128)} %refs_3_.1) | copy-start | bytes 55300
  37.5 37.8 %copy-start = (bf16[1,512,768]{2,1,0:T(8,128)(2,1)S(1)}, bf16[1,512,768]{2,1,0:T(8,128)(2,1)}, u32[]{:S(2)}) copy-start(bf16[1,512,768]{2,1,0:T(8,128)(2,1)} %param.11) | copy-start | bytes 2359300
  74.6 2.1 copy-start.2
  75.3 23.3 %copy-start.22 = (f32[768]{0:T(1024)}, f32[768]{0:T(1024)S(1)}, u32[]{:S(2)}) copy-start(f32[768]{0:T(1024)S(1)} %get-tuple-element.146) | copy-start | bytes 9220
  77.2 21.3 %copy-start.16 = (f32[512]{0:T(512)}, f32[512]{0:T(512)S(1)}, u32[]{:S(2)}) copy-start(f32[512]{0:T(512)S(1)} %add_rsqrt_fusion.1) | copy-start | bytes 6148
  77.3 4.6 %copy-start.31 = (bf16[768,1536]{1,0:T(8,128)(2,1)S(1)}, bf16[768,1536]{1,0:T(8,128)(2,1)}, u32[]{:S(2)}) copy-start(bf16[768,1536]{1,0:T(8,128)(2,1)} %get-tuple-element.89) | copy-start | bytes 7077892
  100.8 2.3 %copy-start.24 = (f32[768]{0:T(1024)S(1)}, f32[768]{0:T(1024)}, u32[]{:S(2)}) copy-start(f32[768]{0:T(1024)} %get-tuple-element.149) | copy-start | bytes 9220
  103.1 2.4 %copy-start.32 = (bf16[768,1536]{1,0:T(8,128)(2,1)S(1)}, bf16[768,1536]{1,0:T(8,128)(2,1)}, u32[]{:S(2)}) copy-start(bf16[768,1536]{1,0:T(8,128)(2,1)} %get-tuple-element.89) | copy-start | bytes 7077892
  103.1 2.4 %copy-start.33 = (f32[512,768]{1,0:T(8,128)S(1)}, f32[512,768]{1,0:T(8,128)}, u32[]{:S(2)}) copy-start(f32[512,768]{1,0:T(8,128)} %get-tuple-element.167) | copy-start | bytes 4718596
  107.2 1.7 copy-start.17
  107.2 1.7 copy-start.23
  146.1 2.3 %copy-start.4 = (bf16[512,768]{1,0:T(8,128)(2,1)S(1)}, bf16[512,768]{1,0:T(8,128)(2,1)}, u32[]{:S(2)}) copy-start(bf16[512,768]{1,0:T(8,128)(2,1)} %get-tuple-element.90) | copy-start | bytes 2359300
  148.3 2.2 copy-start.21
  148.4 2.2 copy-start.20
  152.6 2.4 %copy-start.11 = (bf16[512,192]{0,1:T(8,128)(2,1)S(1)}, bf16[512,192]{0,1:T(8,128)(2,1)}, u32[]{:S(2)}) copy-start(bf16[512,192]{0,1:T(8,128)(2,1)} %copy-done.10) | copy-start | bytes 589828
  152.6 2.3 %copy-start.27 = (f32[3,512]{1,0:T(4,128)S(1)}, f32[3,512]{1,0:T(4,128)}, u32[]{:S(2)}) copy-start(f32[3,512]{1,0:T(4,128)} %copy-done.26) | copy-start | bytes 18436
  152.7 2.3 %copy-start.29 = (pred[512]{0:T(512)(128)(4,1)S(1)}, pred[512]{0:T(512)(128)(4,1)}, u32[]{:S(2)}) copy-start(pred[512]{0:T(512)(128)(4,1)} %copy-done.28) | copy-start | bytes 1540
  161.7 3.0 %copy-start.30 = (f32[768]{0:T(1024)S(1)}, f32[768]{0:T(1024)}, u32[]{:S(2)}) copy-start(f32[768]{0:T(1024)} %get-tuple-element.170) | copy-start | bytes 9220
  165.4 6.6 %copy-start.6 = (bf16[768,768]{1,0:T(8,128)(2,1)S(1)}, bf16[768,768]{1,0:T(8,128)(2,1)}, u32[]{:S(2)}) copy-start(bf16[768,768]{1,0:T(8,128)(2,1)} %get-tuple-element.87) | copy-start | bytes 3538948
  178.8 31.9 %copy-start.15 = (f32[2,6,768]{2,0,1:T(2,128)S(1)}, f32[2,6,768]{2,0,1:T(2,128)}, u32[]{:S(2)}) copy-start(f32[2,6,768]{2,0,1:T(2,128)} %param.21) | copy-start | bytes 110596
  178.8 32.5 %copy-start.25 = (f32[2,6,192]{2,0,1:T(2,128)S(1)}, f32[2,6,192]{2,0,1:T(2,128)}, u32[]{:S(2)}) copy-start(f32[2,6,192]{2,0,1:T(2,128)} %param.20) | copy-start | bytes 27652
  211.9 8.1 %copy-start.9 = (bf16[512,768]{1,0:T(8,128)(2,1)S(1)}, bf16[512,768]{1,0:T(8,128)(2,1)}, u32[]{:S(2)}) copy-start(bf16[512,768]{1,0:T(8,128)(2,1)} %get-tuple-element.91) | copy-start | bytes 2359300
  (10 other events, 12.8 us)

commit v3 on v2

--- a/solution.py
+++ b/solution.py
@@ -44,35 +44,51 @@
 
 
 PIECES = 2
+GATHER_SPLIT = 3
+SCATTER_SPLIT = 4
 PARTS = 4
 
 
-def gather_steps(share_ref, full_ref, local_sem, send_sem, recv_sem):
+def gather_steps(
+    share_ref, full_ref, local_sem, send_sem, recv_sem, first=0, last=RING - 1, pace=1
+):
     me, place, targets = ring_neighbours()
-    rows, columns = share_ref.shape
-    piece_rows, half = rows // PIECES, columns // 2
-
-    def full_at(owner, piece, way):
+    rows, half = full_ref.shape[0] // RING, full_ref.shape[1] // 2
+    piece_rows = rows // PIECES
+
+    def block(ref, owner, piece, way):
         start = pl.multiple_of(owner * rows + piece * piece_rows, piece_rows)
-        return full_ref.at[pl.ds(start, piece_rows), pl.ds(way * half, half)]
-
-    own_start = pl.multiple_of(me * rows, rows)
-    own = pltpu.make_async_copy(share_ref, full_ref.at[pl.ds(own_start, rows)], local_sem)
-    own.start()
+        return ref.at[pl.ds(start, piece_rows), pl.ds(way * half, half)]
+
+    def owner_of(step, way):
+        return ring_device((place + (RING - step if way == 0 else step)) % RING)
+
+    held = []
+    if first == 0:
+        own_start = pl.multiple_of(me * rows, rows)
+        target = full_ref.at[pl.ds(own_start, rows)]
+        held.append(pltpu.make_async_copy(share_ref, target, local_sem.at[0]))
+    else:
+        for step in range(first + 1):
+            for way in range(2):
+                start = pl.multiple_of(owner_of(step, way) * rows, rows)
+                spot = (pl.ds(start, rows), pl.ds(way * half, half))
+                sem = local_sem.at[2 * step + way]
+                held.append(pltpu.make_async_copy(share_ref.at[spot], full_ref.at[spot], sem))
     copies = {}
-    for step in range(RING - 1):
+    for step in range(first, last):
         for piece in range(PIECES):
             for way in range(2):
-                if step:
+                owner = owner_of(step, way)
+                target = source = block(full_ref, owner, piece, way)
+                if step > first:
                     copies[step - 1, piece, way].wait_recv()
-                shift = RING - step if way == 0 else step
-                owner = ring_device((place + shift) % RING)
-                target = full_at(owner, piece, way)
-                source = target
-                if step == 0:
+                elif step == 0:
                     source = share_ref.at[
                         pl.ds(piece * piece_rows, piece_rows), pl.ds(way * half, half)
                     ]
+                else:
+                    source = block(share_ref, owner, piece, way)
                 copy = pltpu.make_async_remote_copy(
                     src_ref=source,
                     dst_ref=target,
@@ -83,38 +99,52 @@
                 )
                 copy.start()
                 copies[step, piece, way] = copy
-        yield
+        if step == first:
+            for copy in held:
+                copy.start()
+        for turn in range(pace):
+            yield
     for (step, piece, way), copy in copies.items():
         copy.wait_send()
-        if step == RING - 2:
+        if step == last - 1:
             copy.wait_recv()
-    own.wait()
-
-
-def scatter_steps(grad_ref, share_ref, arrived, leaving, send_sem, recv_sem):
+    for copy in held:
+        copy.wait()
+
+
+def scatter_steps(
+    grad_ref, end_ref, arrived, leaving, send_sem, recv_sem, carry_ref=None, first=0, last=RING - 1, pace=1
+):
     me, place, targets = ring_neighbours()
-    rows, columns = share_ref.shape
-    piece_rows, half = rows // PIECES, columns // 2
+    rows, half = grad_ref.shape[0] // RING, grad_ref.shape[1] // 2
+    piece_rows = rows // PIECES
+    whole = last == RING - 1
 
     def grad_at(owner, piece, way):
         start = pl.multiple_of(owner * rows + piece * piece_rows, piece_rows)
         return grad_ref.at[pl.ds(start, piece_rows), pl.ds(way * half, half)]
 
     copies = {}
-    for step in range(RING - 1):
+    for step in range(first, last):
         for piece in range(PIECES):
             for way in range(2):
                 shift = RING - 1 - step if way == 0 else 1 + step
                 source = grad_at(ring_device((place + shift) % RING), piece, way)
                 if step:
-                    copies[step - 1, piece, way].wait_recv()
-                    running = arrived[step - 1, piece, way].astype(jnp.float32)
-                    running += source[...].astype(jnp.float32)
+                    if step > first:
+                        copies[step - 1, piece, way].wait_recv()
+                        come = arrived[step - 1, piece, way]
+                    else:
+                        come = carry_ref[piece, way]
+                    running = come.astype(jnp.float32) + source[...].astype(jnp.float32)
                     leaving[step, piece, way] = running.astype(jnp.bfloat16)
                     source = leaving.at[step, piece, way]
+                into = arrived.at[step, piece, way]
+                if step == last - 1 and not whole:
+                    into = end_ref.at[piece, way]
                 copy = pltpu.make_async_remote_copy(
                     src_ref=source,
-                    dst_ref=arrived.at[step, piece, way],
+                    dst_ref=into,
                     send_sem=send_sem.at[step, piece, way],
                     recv_sem=recv_sem.at[step, piece, way],
                     device_id={"dp": targets[way]},
@@ -122,13 +152,15 @@
                 )
                 copy.start()
                 copies[step, piece, way] = copy
-        yield
+        for turn in range(pace):
+            yield
     for piece in range(PIECES):
         for way in range(2):
-            copies[RING - 2, piece, way].wait_recv()
-            total = arrived[RING - 2, piece, way].astype(jnp.float32)
-            total += grad_at(me, piece, way)[...].astype(jnp.float32)
-            share_ref[pl.ds(piece * piece_rows, piece_rows), pl.ds(way * half, half)] = total
+            copies[last - 1, piece, way].wait_recv()
+            if whole:
+                total = arrived[last - 1, piece, way].astype(jnp.float32)
+                total += grad_at(me, piece, way)[...].astype(jnp.float32)
+                end_ref[pl.ds(piece * piece_rows, piece_rows), pl.ds(way * half, half)] = total
     for copy in copies.values():
         copy.wait_send()
 
@@ -228,7 +260,7 @@
     pl.semaphore_wait(barrier, len(ring) + len(tensor))
 
 
-def first_gather_kernel(in_ref, out_ref, full_ref, rest_ref, wide, share, *sems):
+def first_gather_kernel(in_ref, out_ref, full_ref, rest_ref, wide, share, rest, *sems):
     width = in_ref.shape[2]
     for index in range(12):
         if index == 3 or index >= 8:
@@ -237,15 +269,19 @@
             block = in_ref[index if index < 3 else index - 1]
         wide[:, index * width : (index + 1) * width] = block
     share[...] = wide[:, : 4 * width].astype(jnp.bfloat16)
-    rest_ref[...] = wide[:, 4 * width :].astype(jnp.bfloat16)
+    rest[...] = wide[:, 4 * width :].astype(jnp.bfloat16)
     greet_all(ring_neighbours()[2])
-    take_turns(gather_steps(share, full_ref, *sems))
+    take_turns(
+        gather_steps(share, full_ref, *sems[:3]),
+        gather_steps(rest, rest_ref, *sems[3:], last=GATHER_SPLIT, pace=2),
+    )
 
 
 def second_gather_kernel(share_ref, part_ref, full_ref, sum_ref, *scratch):
     greet_all(ring_neighbours()[2], tensor_partners())
     take_turns(
-        gather_steps(share_ref, full_ref, *scratch[:3]), sum_steps(part_ref, sum_ref, *scratch[3:])
+        gather_steps(share_ref, full_ref, *scratch[:3], first=GATHER_SPLIT),
+        sum_steps(part_ref, sum_ref, *scratch[3:]),
     )
 
 
@@ -254,29 +290,47 @@
     take_turns(sum_steps(part_ref, sum_ref, *scratch))
 
 
-def first_scatter_kernel(grad_ref, part_ref, share_ref, sum_ref, *scratch):
+def first_scatter_kernel(grad_ref, part_ref, carry_ref, sum_ref, *scratch):
     greet_all(ring_neighbours()[2], tensor_partners())
     take_turns(
-        scatter_steps(grad_ref, share_ref, *scratch[:4]),
+        scatter_steps(grad_ref, carry_ref, *scratch[:4], last=SCATTER_SPLIT),
         sum_steps(part_ref, sum_ref, *scratch[4:]),
     )
 
 
 def second_scatter_kernel(
-    grad_ref, part_ref, small_ref, share_ref, sum_ref, small_out_ref, *scratch
+    grad_ref,
+    rest_ref,
+    carry_ref,
+    part_ref,
+    small_ref,
+    share_ref,
+    rest_share_ref,
+    sum_ref,
+    small_out_ref,
+    *scratch,
 ):
     me = lax.axis_index("dp")
     greet_all([(me + shift) % RING for shift in range(1, RING)], tensor_partners())
     take_turns(
         scatter_steps(grad_ref, share_ref, *scratch[:4]),
         sum_steps(part_ref, sum_ref, *scratch[4:10]),
-        small_steps(small_ref, small_out_ref, *scratch[10:]),
+        scatter_steps(
+            rest_ref,
+            rest_share_ref,
+            *scratch[13:],
+            carry_ref=carry_ref,
+            first=SCATTER_SPLIT,
+            pace=2,
+        ),
+        small_steps(small_ref, small_out_ref, *scratch[10:13]),
     )
 
 
 def gather_scratch():
     shape = (RING - 1, PIECES, 2)
-    return [pltpu.SemaphoreType.DMA, pltpu.SemaphoreType.DMA(shape), pltpu.SemaphoreType.DMA(shape)]
+    sems = pltpu.SemaphoreType.DMA(shape)
+    return [pltpu.SemaphoreType.DMA((2 * RING,)), sems, sems]
 
 
 def scatter_scratch(rows, columns):
@@ -325,12 +379,14 @@
             (in_weight, out_weight),
             [
                 ((RING * rows, 4 * group_width), jnp.bfloat16),
-                ((rows, 8 * group_width), jnp.bfloat16),
+                ((RING * rows, 8 * group_width), jnp.bfloat16),
             ],
             [
                 pltpu.VMEM((rows, 12 * group_width), jnp.float32),
                 pltpu.VMEM((rows, 4 * group_width), jnp.bfloat16),
+                pltpu.VMEM((rows, 8 * group_width), jnp.bfloat16),
             ]
+            + gather_scratch()
             + gather_scratch(),
             0,
         )
@@ -348,13 +404,12 @@
     return lax.psum(part, "tensor")
 
 
-def gather_second(rest, part):
-    rows, columns = rest.shape
+def gather_second(rows, rest, part):
     if ring_here(rows):
         return kernel_call(
             second_gather_kernel,
             (rest, part),
-            [((RING * rows, columns), jnp.bfloat16), (part.shape, jnp.bfloat16)],
+            [(rest.shape, jnp.bfloat16), (part.shape, jnp.bfloat16)],
             gather_scratch() + sum_scratch(*part.shape),
             2,
         )
@@ -372,28 +427,35 @@
         return kernel_call(
             first_scatter_kernel,
             (grads, part),
-            [((rows, columns), jnp.float32), (part.shape, jnp.bfloat16)],
+            [
+                ((PIECES, 2, rows // PIECES, columns // 2), jnp.bfloat16),
+                (part.shape, jnp.bfloat16),
+            ],
             scatter_scratch(rows, columns) + sum_scratch(*part.shape),
             3,
         )
     return scatter_plain(grads), lax.psum(part, "tensor")
 
 
-def scatter_second(grads, part, small):
+def scatter_second(grads, rest, carry, part, small):
     rows, columns = grads.shape[0] // lax.axis_size("dp"), grads.shape[1]
     if ring_here(rows):
         return kernel_call(
             second_scatter_kernel,
-            (grads, part, small),
+            (grads, rest, carry, part, small),
             [
                 ((rows, columns), jnp.float32),
+                ((rows, rest.shape[1]), jnp.float32),
                 (part.shape, jnp.bfloat16),
                 (small.shape, jnp.float32),
             ],
-            scatter_scratch(rows, columns) + sum_scratch(*part.shape) + small_scratch(small),
+            scatter_scratch(rows, columns)
+            + sum_scratch(*part.shape)
+            + small_scratch(small)
+            + scatter_scratch(rows, rest.shape[1]),
             4,
         )
-    return scatter_plain(grads), lax.psum(part, "tensor"), lax.psum(small, "dp")
+    return scatter_plain(grads), carry, lax.psum(part, "tensor"), lax.psum(small, "dp")
 
 
 def matmul(left_op, right_op):
@@ -590,7 +652,7 @@
     )
     mixed_flat = mixed_heads.reshape(row_count, group_width)
     attn_part = times_transposed(mixed_flat, w_proj).astype(jnp.bfloat16)
-    second_full, attn_out = gather_second(rest, attn_part)
+    second_full, attn_out = gather_second(in_weight.shape[1], rest, attn_part)
     w_up = second_full[:, : 4 * group_width]
     w_down = second_full[:, 4 * group_width :]
     hidden, normed_one, inverse_one = layer_norm(
@@ -616,7 +678,7 @@
     grad_up = inner_rows(hidden_low, grad_pre_low).astype(jnp.bfloat16)
     rest_grads = jnp.concatenate([grad_up, grad_down], 1)
     back_part = times_transposed(grad_pre_low, w_up).astype(jnp.bfloat16)
-    rest_total, back_sum = scatter_first(rest_grads, back_part)
+    carry, back_sum = scatter_first(rest_grads, back_part)
     grad_hidden = grad_two + back_sum.astype(jnp.float32)
     grad_one = norm_back(grad_hidden, normed_one, inverse_one, norm_vec[1])
     grad_one_low = grad_one.astype(jnp.bfloat16)
@@ -654,7 +716,9 @@
         ]
     )
     small = jnp.pad(jnp.concatenate([norm_rows, bias_rows], 1), ((0, 2), (0, 64)))
-    share_total, input_sum, small_total = scatter_second(first_grads, input_part, small)
+    share_total, rest_total, input_sum, small_total = scatter_second(
+        first_grads, rest_grads, carry, input_part, small
+    )
     grad_input = grad_one + input_sum.astype(jnp.float32)
     params = (in_weight, out_weight, in_bias, norm_vec)
     moments = (in_moments, out_moments, bias_moments, norm_moments)

time: 222 us -> 208 us (0.937)
  Pallas kernels: 150 us -> 137 us
    pallas_call x6, Pallas kernels: 150 us -> 137 us  [kernel_call(): pl.pallas_call(kernel, out_shape=tuple((jax.ShapeDtypeStruct(shape, dtype...]
where the time goes in v3:
time: 208 us
  Pallas kernels  137 us (66%)
  matrix products  41.1 us (20%)
  other arithmetic  17.8 us (9%)
  local copies, waits for them, and re-layouts  9.75 us (5%)
    pallas_call x6, Pallas kernels, kernel_call(): pl.pallas_call(kernel, out_shape=tuple((jax.ShapeDtypeStruct(shape, dtype...  137 us
    dot_general x4, matrix products, matmul(): return jnp.dot(left_op, right_op, preferred_element_type=jnp.float32)  9.67 us
    dot_general x4, matrix products, times_transposed(): lax.dot_general(left_op, right_op, (((1,), (1,)), ((), ())), preferred_el...  7.6 us
    unnamed x72, local copies, waits for them, and re-layouts  6.78 us
    dot_general x1, matrix products, attend_backward(): jnp.einsum('hqk,qhe->khe', grad_scores, query_heads, preferred_element_ty...  6.64 us
    dot_general x1, matrix products, attend_backward(): jnp.einsum('hqk,khe->qhe', grad_scores, key_heads, preferred_element_type...  6.59 us

profile of v3, /device:TPU:0, one launch (start us, length us, event | category | flops | bytes accessed | tf_op | source)
XLA Modules:
  0.0 207.8 jit_solution(17407288047408881405)
XLA Ops:
  0.6 34.0 %shard_map.218 = (bf16[768,768]{1,0:T(8,128)(2,1)}, bf16[768,1536]{1,0:T(8,128)(2,1)}) custom-call(f32[7,96,192]{2,1,0:T(8,128)} %refs_0_.1, f32[5,192,96]{2,1,0:T(8,128)} %refs_1_.1), custom_call_target="tpu_custom_call" | custom-call | tf_op jit(solution)/shard_map/pallas_call | solution.py:356
  34.7 2.2 %convolution_bitcast_fusion = f32[512,576]{0,1:T(8,128)S(1)} fusion(bf16[768,768]{1,0:T(8,128)(2,1)} %get-tuple-element.88, bf16[1,512,768]{2,1,0:T(8,128)(2,1)} %param.11), kind=kOutput, calls=%fused_computation.49 | convolution fusion | flops 452984832 | bytes 2949120 | tf_op jit(solution)/shard_map/dot_general | solution.py:462
  41.1 2.5 %convolution_convert_fusion.6.part_ref = bf16[512,768]{1,0:T(8,128)(2,1)} fusion(bf16[512,192]{0,1:T(8,128)(2,1)S(1)} %bitcast.83, bf16[768,768]{1,0:T(8,128)(2,1)} %get-tuple-element.88), kind=kOutput, calls=%fused_computation.53 | convolution fusion | flops 151388160 | bytes 1376256 | tf_op jit(solution)/shard_map/dot_general | solution.py:472
  43.6 22.8 %shard_map.219 = (bf16[768,1536]{1,0:T(8,128)(2,1)}, bf16[512,768]{1,0:T(8,128)(2,1)}) custom-call(bf16[768,1536]{1,0:T(8,128)(2,1)} %get-tuple-element.87.share_ref, bf16[512,768]{1,0:T(8,128)(2,1)} %convolution_convert_fusion.6.part_ref), custom_call_target="tpu_custom_call" | custom-call | tf_op jit(solution)/shard_map/pallas_call | solution.py:356
  69.1 3.7 %multiply_convert_fusion.1 = (bf16[512,768]{1,0:T(8,128)(2,1)S(1)}, f32[512,768]{1,0:T(8,128)}) fusion(f32[768]{0:T(1024)S(1)} %add.135, bf16[768,1536]{1,0:T(8,128)(2,1)} %get-tuple-element.90, f32[768]{0:T(1024)S(1)} %get-tuple-element.148, f32[768]{0:T(1024)S(1)} %get-tuple-element.149, f32[512]{0:T(512)S(1)} %add_rsqrt_fusion.1, ...), kind=kOutput, calls=%fused_computation.36 | convolution fusion | flops 609878016 | bytes 5128192 | tf_op jit(solution)/shard_map/dot_general | solution.py:462
  73.8 1.7 convolution_convert_fusion.4.part_ref
  75.4 15.3 %shard_map.220 = bf16[512,768]{1,0:T(8,128)(2,1)} custom-call(bf16[512,768]{1,0:T(8,128)(2,1)} %convolution_convert_fusion.4.part_ref), custom_call_target="tpu_custom_call" | custom-call | tf_op jit(solution)/shard_map/pallas_call | solution.py:356
  90.8 1.9 fusion.69
  95.4 2.4 %fusion.23 = (f32[512,768]{1,0:T(8,128)S(1)}, bf16[1,512,768]{2,1,0:T(8,128)(2,1)}) fusion(f32[512,768]{1,0:T(8,128)S(1)} %get-tuple-element.155, bf16[1,512,768]{2,1,0:T(8,128)(2,1)S(1)} %copy-done.5, f32[512]{0:T(512)S(1)} %broadcast_multiply_fusion.2, f32[512]{0:T(512)S(1)} %broadcast_multiply_fusion.3, f32[512]{0:T(512)} %copy-done.19, ...), kind=kLoop, calls=%fused_computation.25 | loop fusion | flops 4718592 | bytes 4734976 | tf_op jit(solution)/shard_map/mul | solution.py:487
  97.8 1.7 fusion.75
  99.5 1.7 convolution_convert_fusion.3.part_ref
  103.1 1.6 pad_maximum_fusion.grad_ref.rest_ref
  104.7 21.3 %shard_map.221 = (bf16[2,2,48,768]{3,2,1,0:T(8,128)(2,1)}, bf16[512,768]{1,0:T(8,128)(2,1)}) custom-call(bf16[768,1536]{1,0:T(8,128)(2,1)} %pad_maximum_fusion.grad_ref.rest_ref, bf16[512,768]{1,0:T(8,128)(2,1)} %convolution_convert_fusion.3.part_ref), custom_call_target="tpu_custom_call" | custom-call | tf_op jit(solution)/shard_map/pallas_call | solution.py:356
  126.0 2.2 %multiply_reduce_fusion.1 = (f32[768]{0:T(1024)S(1)}, f32[512]{0:T(512)S(1)}, f32[512]{0:T(512)S(1)}, f32[768]{0:T(1024)S(1)}, f32[768]{0:T(1024)S(1)}) fusion(f32[512,768]{1,0:T(8,128)S(1)} %get-tuple-element.156, bf16[512,768]{1,0:T(8,128)(2,1)} %get-tuple-element.91, f32[512]{0:T(512)S(1)} %copy-done.17, f32[512]{0:T(512)S(1)} %broadcast_multiply_fusion.5, ...), kind=kLoop, calls=%fused_computation.29 | loop fusion | flops 6288128 | bytes 3955712 | tf_op jit(solution)/shard_map/reduce_sum | solution.py:711
  128.3 2.2 %fusion.68 = (f32[768]{0:T(1024)S(1)}, f32[512,768]{1,0:T(8,128)}) fusion(f32[512]{0:T(512)S(1)} %broadcast_multiply_fusion, f32[512]{0:T(512)S(1)} %broadcast_multiply_fusion.5, f32[768]{0:T(1024)S(1)} %get-tuple-element.150, bf16[512,768]{1,0:T(8,128)(2,1)S(1)} %copy-done.2, bf16[1,512,768]{2,1,0:T(8,128)(2,1)S(1)} %copy-done, ...), kind=kLoop, calls=%fused_computation.117 | loop fusion | flops 5504256 | bytes 5522432 | tf_op jit(solution)/shard_map/reduce_sum | solution.py:710
  130.6 2.0 convolution_convert_fusion.8
  132.7 2.3 %fusion.76 = f32[3,512,512]{1,2,0:T(8,128)} fusion(bf16[512,3,64]{0,2,1:T(8,128)(2,1)S(1)} %bitcast.77, bf16[512,3,64]{0,2,1:T(8,128)(2,1)S(1)} %bitcast.76), kind=kOutput, calls=%fused_computation.123 | convolution fusion | flops 100663296 | bytes 3538944 | tf_op jit(solution)/shard_map/while/body/eval_jaxpr/qhe,khe->hqk/dot_general | solution.py:534
  135.0 6.6 %fusion.71 = (f32[3,64]{1,0:T(4,128)S(1)}, bf16[512,3,64]{0,2,1:T(8,128)(2,1)S(1)}) fusion(bf16[512,3,64]{0,2,1:T(8,128)(2,1)S(1)} %bitcast.82, f32[3,512,512]{1,2,0:T(8,128)} %fusion.76, f32[3,512]{1,0:T(4,128)S(1)} %copy-done.27, f32[3,512,512]{1,2,0:T(8,128)} %copy-done.3, pred[512]{0:T(512)(128)(4,1)S(1)} %copy-done.29), kind=kOutput, calls=%fused_computation.120 | convolution fusion | flops 109512512 | bytes 6692096 | tf_op jit(solution)/shard_map/while/body/eval_jaxpr/hqk,khe->qhe/dot_general | solution.py:539
  141.7 2.9 %fusion.70 = (f32[3,64]{1,0:T(4,128)S(1)}, bf16[512,3,64]{0,2,1:T(8,128)(2,1)S(1)}) fusion(bf16[512,3,64]{0,2,1:T(8,128)(2,1)S(1)} %bitcast.78, f32[3,512]{1,0:T(4,128)S(1)} %copy-done.27, f32[3,512,512]{1,2,0:T(8,128)} %copy-done.3, pred[512]{0:T(512)(128)(4,1)S(1)} %copy-done.29), kind=kOutput, calls=%fused_computation.119 | convolution fusion | flops 104005440 | bytes 3546368 | tf_op jit(solution)/shard_map/while/body/eval_jaxpr/hqk,qhe->khe/dot_general | solution.py:545
  145.4 6.6 %fusion.33 = bf16[3,64,512]{2,1,0:T(8,128)(2,1)S(1)} fusion(bf16[512,3,64]{0,2,1:T(8,128)(2,1)S(1)} %bitcast.80, f32[3,512,512]{1,2,0:T(8,128)} %fusion.76, f32[3,512,512]{1,2,0:T(8,128)} %copy-done.3, f32[3,512]{1,0:T(4,128)S(1)} %copy-done.27, pred[512]{0:T(512)(128)(4,1)S(1)} %copy-done.29), kind=kOutput, calls=%fused_computation.61 | convolution fusion | flops 109414400 | bytes 6691328 | tf_op jit(solution)/shard_map/while/body/eval_jaxpr/hqk,qhe->khe/dot_general | solution.py:542
  152.1 1.7 convolution_convert_fusion.5.part_ref
  155.3 1.7 copy.43
  158.8 38.7 %shard_map.222 = (f32[96,768]{1,0:T(8,128)}, f32[96,1536]{1,0:T(8,128)}, bf16[512,768]{1,0:T(8,128)(2,1)}, f32[8,1024]{1,0:T(8,128)}) custom-call(bf16[768,768]{1,0:T(8,128)(2,1)} %pad_maximum_fusion.1.grad_ref, bf16[768,1536]{1,0:T(8,128)(2,1)} %pad_maximum_fusion.grad_ref.rest_ref, bf16[2,2,48,768]{3,2,1,0:T(8,128)(2,1)} %get-tuple-element.92.carry_ref, ...), custom_call_target="tpu_custom_call" | custom-call | tf_op jit(solution)/shard_map/pallas_call | solution.py:356
  198.7 5.3 %shard_map.223 = (f32[7,96,192]{2,1,0:T(8,128)}, f32[5,192,96]{2,1,0:T(8,128)}, f32[6,192]{1,0:T(8,128)}, f32[6,768]{1,0:T(8,128)}, f32[7,96,192]{2,1,0:T(8,128)...) custom-call(f32[96,768]{1,0:T(8,128)} %get-tuple-element.94.share_re, ...), custom_call_target="tpu_custom_call" | custom-call | tf_op jit(solution)/shard_map/pallas_call | solution.py:356
  (114 shorter events, 20.9 us)
Async XLA Ops:
  34.7 2.2 %copy-start.18 = (f32[6,192]{1,0:T(8,128)S(1)}, f32[6,192]{1,0:T(8,128)}, u32[]{:S(2)}) copy-start(f32[6,192]{1,0:T(8,128)} %refs_2_.1) | copy-start | bytes 13828
  37.8 55.3 %copy-start.19 = (f32[512]{0:T(512)}, f32[512]{0:T(512)S(1)}, u32[]{:S(2)}) copy-start(f32[512]{0:T(512)S(1)} %get-tuple-element.175) | copy-start | bytes 6148
  39.3 1.8 copy-start.26
  41.1 2.5 %copy-start.12 = (bf16[3,64,512]{2,1,0:T(8,128)(2,1)}, bf16[3,64,512]{2,1,0:T(8,128)(2,1)S(1)}, u32[]{:S(2)}) copy-start(bf16[3,64,512]{2,1,0:T(8,128)(2,1)S(1)} %convolution_convert_fusion.9) | copy-start | bytes 589828
  43.6 22.8 %copy-start.14 = (f32[6,768]{1,0:T(8,128)S(1)}, f32[6,768]{1,0:T(8,128)}, u32[]{:S(2)}) copy-start(f32[6,768]{1,0:T(8,128)} %refs_3_.1) | copy-start | bytes 55300
  43.6 23.5 %copy-start = (bf16[1,512,768]{2,1,0:T(8,128)(2,1)S(1)}, bf16[1,512,768]{2,1,0:T(8,128)(2,1)}, u32[]{:S(2)}) copy-start(bf16[1,512,768]{2,1,0:T(8,128)(2,1)} %param.11) | copy-start | bytes 2359300
  66.4 2.1 %copy-start.2 = (bf16[512,768]{1,0:T(8,128)(2,1)S(1)}, bf16[512,768]{1,0:T(8,128)(2,1)}, u32[]{:S(2)}) copy-start(bf16[512,768]{1,0:T(8,128)(2,1)} %get-tuple-element.89) | copy-start | bytes 2359300
  67.1 23.7 %copy-start.22 = (f32[768]{0:T(1024)}, f32[768]{0:T(1024)S(1)}, u32[]{:S(2)}) copy-start(f32[768]{0:T(1024)S(1)} %get-tuple-element.148) | copy-start | bytes 9220
  69.0 21.8 %copy-start.16 = (f32[512]{0:T(512)}, f32[512]{0:T(512)S(1)}, u32[]{:S(2)}) copy-start(f32[512]{0:T(512)S(1)} %add_rsqrt_fusion.1) | copy-start | bytes 6148
  69.1 4.6 %copy-start.31 = (bf16[768,1536]{1,0:T(8,128)(2,1)S(1)}, bf16[768,1536]{1,0:T(8,128)(2,1)}, u32[]{:S(2)}) copy-start(bf16[768,1536]{1,0:T(8,128)(2,1)} %get-tuple-element.90) | copy-start | bytes 7077892
  93.1 2.3 %copy-start.24 = (f32[768]{0:T(1024)S(1)}, f32[768]{0:T(1024)}, u32[]{:S(2)}) copy-start(f32[768]{0:T(1024)} %get-tuple-element.151) | copy-start | bytes 9220
  95.3 2.4 %copy-start.32 = (bf16[768,1536]{1,0:T(8,128)(2,1)S(1)}, bf16[768,1536]{1,0:T(8,128)(2,1)}, u32[]{:S(2)}) copy-start(bf16[768,1536]{1,0:T(8,128)(2,1)} %get-tuple-element.90) | copy-start | bytes 7077892
  95.3 2.4 %copy-start.33 = (f32[512,768]{1,0:T(8,128)S(1)}, f32[512,768]{1,0:T(8,128)}, u32[]{:S(2)}) copy-start(f32[512,768]{1,0:T(8,128)} %get-tuple-element.169) | copy-start | bytes 4718596
  126.0 2.3 %copy-start.4 = (bf16[512,768]{1,0:T(8,128)(2,1)S(1)}, bf16[512,768]{1,0:T(8,128)(2,1)}, u32[]{:S(2)}) copy-start(bf16[512,768]{1,0:T(8,128)(2,1)} %get-tuple-element.91) | copy-start | bytes 2359300
  128.3 2.2 %copy-start.21 = (f32[768]{0:T(1024)S(1)}, f32[768]{0:T(1024)}, u32[]{:S(2)}) copy-start(f32[768]{0:T(1024)} %get-tuple-element.139) | copy-start | bytes 9220
  128.3 2.2 %copy-start.20 = (f32[768]{0:T(1024)S(1)}, f32[768]{0:T(1024)}, u32[]{:S(2)}) copy-start(f32[768]{0:T(1024)} %get-tuple-element.145) | copy-start | bytes 9220
  132.6 2.4 %copy-start.11 = (bf16[512,192]{0,1:T(8,128)(2,1)S(1)}, bf16[512,192]{0,1:T(8,128)(2,1)}, u32[]{:S(2)}) copy-start(bf16[512,192]{0,1:T(8,128)(2,1)} %copy-done.10) | copy-start | bytes 589828
  132.6 2.3 %copy-start.27 = (f32[3,512]{1,0:T(4,128)S(1)}, f32[3,512]{1,0:T(4,128)}, u32[]{:S(2)}) copy-start(f32[3,512]{1,0:T(4,128)} %copy-done.26) | copy-start | bytes 18436
  132.7 2.3 %copy-start.29 = (pred[512]{0:T(512)(128)(4,1)S(1)}, pred[512]{0:T(512)(128)(4,1)}, u32[]{:S(2)}) copy-start(pred[512]{0:T(512)(128)(4,1)} %copy-done.28) | copy-start | bytes 1540
  141.7 3.0 %copy-start.30 = (f32[768]{0:T(1024)S(1)}, f32[768]{0:T(1024)}, u32[]{:S(2)}) copy-start(f32[768]{0:T(1024)} %get-tuple-element.172) | copy-start | bytes 9220
  145.4 6.6 %copy-start.6 = (bf16[768,768]{1,0:T(8,128)(2,1)S(1)}, bf16[768,768]{1,0:T(8,128)(2,1)}, u32[]{:S(2)}) copy-start(bf16[768,768]{1,0:T(8,128)(2,1)} %get-tuple-element.88) | copy-start | bytes 3538948
  158.8 38.7 %copy-start.15 = (f32[2,6,768]{2,0,1:T(2,128)S(1)}, f32[2,6,768]{2,0,1:T(2,128)}, u32[]{:S(2)}) copy-start(f32[2,6,768]{2,0,1:T(2,128)} %param.21) | copy-start | bytes 110596
  158.8 39.4 %copy-start.25 = (f32[2,6,192]{2,0,1:T(2,128)S(1)}, f32[2,6,192]{2,0,1:T(2,128)}, u32[]{:S(2)}) copy-start(f32[2,6,192]{2,0,1:T(2,128)} %param.20) | copy-start | bytes 27652
  198.7 8.1 %copy-start.9 = (bf16[512,768]{1,0:T(8,128)(2,1)S(1)}, bf16[512,768]{1,0:T(8,128)(2,1)}, u32[]{:S(2)}) copy-start(bf16[512,768]{1,0:T(8,128)(2,1)} %get-tuple-element.93) | copy-start | bytes 2359300
  (10 other events, 14.6 us)
